TPU v7x, 256 devices: a whole 4x4x8 slice. The times are simulated.
256 devices in a mesh: apa: 16 (over z, core), slab: 4 (over x), band: 4 (over y).
Axes of the slice: x: 4, y: 4, z: 8, core: 2. Of those that a mesh axis runs over, the one named last changes fastest.
Arguments:
- raw: bfloat16 [32, 2560, 1024], P('apa', 'band', 'slab'), may hold values from -6 to 6
- dead_mask: int32 [32, 2560], P('apa', 'band'), may hold values 0 or 1
- kernel: bfloat16 [21, 257], replicated, may hold values from -0.078125 to 0.078125
- blob_wires: int32 [49152, 12], P(('apa', 'band')), may hold values from -1 to 81919, as said below
Outputs:
- signal: bfloat16 [32, 2560, 1024], P('apa', 'band', 'slab')
- blob_charge: float32 [49152, 512], P(('apa', 'band'), 'slab')
Inputs may be any that keep to these rules, and one draw needn't show every extreme that they name: `blob_wires`: each entry is -1 or a wire a * 2560 + w of the whole detector. The owner of blob b is the device b // 768 in the order of apa+band. The wires named by one owner's blobs are distinct, and at most 128 of them are held by any one device (one band of its 2 APAs); in every draw some owner names exactly 128 from every such device.
All inputs are finite; a program needn't handle non-finite values. No bound on the sum of `dead_mask` on one device may be relied on, other than what follows from the above.
Results may differ from a plain program's by a relative error of at most 0.0051.
Values may be sent and summed in bfloat16 or wider, within the bound.
A program may use at most 128 MiB of HBM per device.

v0:
```python
import math

import jax
import jax.numpy as jnp
from jax import lax
from jax.sharding import PartitionSpec as P

W = 2560
WR = 10
H = 128
ROWS_PEER = 128


def with_halo(block, sides, width):
    for axis, dim in sides:
        count = lax.axis_size(axis)
        forward = [(i, i + 1) for i in range(count - 1)]
        backward = [(target, source) for source, target in forward]
        low = lax.ppermute(
            lax.slice_in_dim(block, block.shape[dim] - width, None, axis=dim), axis, forward
        )
        high = lax.ppermute(lax.slice_in_dim(block, 0, width, axis=dim), axis, backward)
        block = jnp.concatenate([low, block, high], axis=dim)
    return block


def running_counts(hits):
    entries, groups = hits.shape
    block = math.gcd(entries, 128)
    blocks = entries // block
    stacked = hits.reshape(blocks, block, groups)
    inner_index = jnp.arange(block, dtype=jnp.int32)
    lower = (inner_index[:, None] >= inner_index[None, :]).astype(jnp.float32)
    inside = jnp.einsum(
        "ij,bjg->big",
        lower,
        stacked,
        precision=lax.Precision.HIGHEST,
        preferred_element_type=jnp.float32,
    )
    block_index = jnp.arange(blocks, dtype=jnp.int32)
    before = (block_index[:, None] > block_index[None, :]).astype(jnp.float32)
    offsets = jnp.dot(
        before,
        jnp.sum(stacked, axis=1),
        precision=lax.Precision.HIGHEST,
        preferred_element_type=jnp.float32,
    )
    return (inside + offsets[:, None, :]).reshape(entries, groups)


def shards(raw, dead_mask, kernel, blob_wires):
    apa_count, band_wires, slab_ticks = raw.shape
    length = slab_ticks + 2 * H
    clean = raw * dead_mask.astype(jnp.bfloat16)[:, :, None]
    extended = with_halo(clean, (("slab", 2),), H)
    widened = with_halo(extended, (("band", 1),), WR)
    source_tick = jnp.arange(length, dtype=jnp.int32)
    target_tick = jnp.arange(slab_ticks, dtype=jnp.int32)
    tap_place = target_tick[None, :] - source_tick[:, None] + 2 * H
    valid_tap = (tap_place >= 0) & (tap_place <= 2 * H)
    tap_clipped = jnp.clip(tap_place, 0, 2 * H)
    tables = jnp.where(valid_tap[None, :, :], kernel[:, tap_clipped], jnp.zeros((), jnp.bfloat16))
    total = jnp.zeros((apa_count * band_wires, slab_ticks), jnp.float32)
    for offset in range(2 * WR + 1):
        shifted = widened[:, offset : offset + band_wires].reshape(apa_count * band_wires, length)
        total = total + jnp.dot(shifted, tables[offset], preferred_element_type=jnp.float32)
    signal = total.reshape(apa_count, band_wires, slab_ticks).astype(jnp.bfloat16)
    slice_count = slab_ticks // 2
    slice_rows = (
        signal.astype(jnp.float32).reshape(apa_count, band_wires, slice_count, 2).sum(axis=3)
    )
    slice_rows = slice_rows.astype(jnp.bfloat16).reshape(apa_count * band_wires, slice_count)
    apa_size = lax.axis_size("apa")
    band_count = lax.axis_size("band")
    groups = apa_size * band_count
    blob_count, places = blob_wires.shape
    wire_refs = blob_wires.reshape(-1)
    usable = wire_refs >= 0
    global_wire = jnp.where(usable, wire_refs, 0)
    apa_number = global_wire // W
    wire_number = global_wire % W
    source = apa_number // apa_count * band_count + wire_number // band_wires
    local_row = apa_number % apa_count * band_wires + wire_number % band_wires
    source_hot = (
        (source[:, None] == jnp.arange(groups, dtype=jnp.int32)[None, :]) & usable[:, None]
    ).astype(jnp.float32)
    counted = running_counts(source_hot)
    slot_index = jnp.sum(source_hot * (counted - 1.0), axis=1).astype(jnp.int32)
    slot_hot = (
        (slot_index[:, None] == jnp.arange(ROWS_PEER, dtype=jnp.int32)[None, :]) & usable[:, None]
    ).astype(jnp.float32)
    row_value = (local_row + 1).astype(jnp.float32)
    request = jnp.dot(
        (source_hot * row_value[:, None]).T,
        slot_hot,
        precision=lax.Precision.HIGHEST,
        preferred_element_type=jnp.float32,
    )
    request = request.astype(jnp.int32) - 1
    asked_rows = lax.all_to_all(request, ("apa", "band"), split_axis=0, concat_axis=0, tiled=True)
    held_rows = jnp.arange(apa_count * band_wires, dtype=jnp.int32)
    pick_table = (asked_rows[:, :, None] == held_rows[None, None, :]).astype(jnp.bfloat16)
    outgoing = jnp.einsum("gsr,rt->gst", pick_table, slice_rows, preferred_element_type=jnp.float32)
    outgoing = outgoing.astype(jnp.bfloat16)
    incoming = lax.all_to_all(outgoing, ("apa", "band"), split_axis=0, concat_axis=0, tiled=True)
    incoming = incoming.reshape(groups * ROWS_PEER, slice_count)
    placement = jnp.einsum(
        "bkg,bks->bgs",
        source_hot.reshape(blob_count, places, groups),
        slot_hot.reshape(blob_count, places, ROWS_PEER),
        precision=lax.Precision.HIGHEST,
        preferred_element_type=jnp.float32,
    )
    placement = placement.reshape(blob_count, groups * ROWS_PEER).astype(jnp.bfloat16)
    blob_charge = jnp.dot(placement, incoming, preferred_element_type=jnp.float32)
    return (signal, blob_charge)


def solution(mesh):
    return jax.shard_map(
        shards,
        mesh=mesh,
        in_specs=(P("apa", "band", "slab"), P("apa", "band"), P(), P(("apa", "band"), None)),
        out_specs=(P("apa", "band", "slab"), P(("apa", "band"), "slab")),
        check_vma=False,
    )
```

profile of v0, /device:TPU:1, one launch (start us, length us, event | category | flops | bytes accessed | tf_op | source)
XLA Modules:
  0.0 628.4 jit_solution(18330034808578844200)
XLA Ops:
  0.6 0.7 convert_element_type.59
  1.3 1.3 broadcast_multiply_fusion
  2.8 4.0 collective-permute-start
  6.8 1.3 collective-permute-start.1
  9.1 0.9 convert_reduce_fusion
  10.1 1.3 fusion.17
  11.4 0.6 fusion.84
  12.0 3.9 fusion.43
  15.9 12.8 %all-to-all-start = ((s32[64,1,128]{2,1,0:T(1,128)}), s32[64,1,128]{2,1,0:T(1,128)}, u32[]{:S(2)}, u32[]{:S(2)}) async-start(s32[64,1,128]{2,1,0:T(1,128)} %bitcast.49), calls=%async_computation | async-start | bytes 65536 | tf_op jit(solution)/shard_map/all_to_all | solution.py:101
  29.6 457.0 %gather_fusion = bf16[131072,21]{1,0:T(8,128)(2,1)} fusion(bf16[21,257]{0,1:T(8,128)(2,1)S(1)} %copy.32, s32[131072]{0:T(1024)S(1)} %broadcast_clamp_fusion), kind=kCustom, calls=%fused_computation | custom fusion | bytes 11534336 | tf_op jit(solution)/shard_map/gather | solution.py:63
  486.6 26.8 %copy.33 = bf16[512,256,21]{1,0,2:T(8,128)(2,1)} copy(bf16[512,256,21]{2,1,0:T(8,128)(2,1)} %bitcast.136) | data formatting | bytes 11010048 | tf_op jit(solution)/shard_map/gather | solution.py:63
  513.6 3.3 collective-permute-start.2
  516.9 1.5 collective-permute-start.3
  518.4 3.3 select_bitcast_fusion
  521.7 0.6 maximum_maximum_fusion
  522.3 3.7 fusion.81
  526.0 3.3 fusion.80
  529.3 1.9 fusion.53
  531.2 0.5 fusion.52
  531.8 0.8 copy-done.2
  532.6 0.5 convolution_add_fusion.18
  533.1 0.8 copy-done.1
  533.9 0.5 convolution_add_fusion.17
  534.4 0.8 copy-done
  535.2 0.5 convolution_add_fusion.16
  535.7 0.5 convolution_add_fusion.15
  536.2 0.5 convolution_add_fusion.14
  536.7 0.5 convolution_add_fusion.13
  537.2 0.5 convolution_add_fusion.12
  537.7 0.5 convolution_add_fusion.11
  538.3 0.5 convolution_add_fusion.10
  538.8 0.5 fusion.15
  539.3 0.5 convolution_add_fusion.8
  539.8 0.5 convolution_add_fusion.7
  540.3 0.5 convolution_add_fusion.6
  540.8 0.5 convolution_add_fusion.5
  541.4 0.5 convolution_add_fusion.4
  541.9 0.5 convolution_add_fusion.3
  542.4 0.5 convolution_add_fusion.2
  542.9 0.5 convolution_add_fusion.1
  543.4 0.5 fusion.16
  544.3 1.2 reduce_sum.32
  545.6 0.7 copy.46
  546.3 10.2 %fusion.28 = bf16[64,128,128]{2,1,0:T(8,128)(2,1)} fusion(bf16[1280,128,1]{1,0,2:T(8,128)(2,1)S(1)} %bitcast.160, s32[64,128]{1,0:T(8,128)} %bitcast.50), kind=kOutput, calls=%fused_computation.51 | convolution fusion | flops 2695888896 | bytes 2457600 | tf_op jit(solution)/shard_map/gsr,rt->gst/dot_general | solution.py:104
  556.4 11.7 %all-to-all-start.1 = ((bf16[64,128,128]{2,1,0:T(8,128)(2,1)}), bf16[64,128,128]{2,1,0:T(8,128)(2,1)S(1)}, u32[]{:S(2)}, u32[]{:S(2)}) async-start(bf16[64,128,128]{2,1,0:T(8,128)(2,1)} %fusion.28), calls=%async_computation.1 | async-start | bytes 4194304 | tf_op jit(solution)/shard_map/all_to_all | solution.py:106
  569.1 21.2 %convolution_convert_fusion = bf16[768,64,128]{2,1,0:T(8,128)(2,1)} fusion(s32[768,12]{1,0:T(8,128)S(1)} %convert_element_type.64, s32[768,12]{1,0:T(8,128)S(1)} %copy.34, pred[768,12]{1,0:T(8,128)(4,1)S(1)} %copy.35), kind=kOutput, calls=%fused_computation.6 | convolution fusion | flops 160825344 | bytes 12665856 | tf_op jit(solution)/shard_map/bkg,bks->bgs/dot_general | solution.py:108
  590.3 27.7 %all-to-all-done.1 = bf16[64,128,128]{2,1,0:T(8,128)(2,1)S(1)} async-done(((bf16[64,128,128]{2,1,0:T(8,128)(2,1)}), bf16[64,128,128]{2,1,0:T(8,128)(2,1)S(1)}, u32[]{:S(2)}, u32[]{:S(2)}) %all-to-all-start.1) | async-done | bytes 2097184 | tf_op jit(solution)/shard_map/all_to_all | solution.py:106
  618.0 10.4 %fusion.29 = f32[768,128]{1,0:T(8,128)} fusion(bf16[64,128,128]{2,1,0:T(8,128)(2,1)S(1)} %all-to-all-done.1, bf16[768,64,128]{2,1,0:T(8,128)(2,1)} %convolution_convert_fusion), kind=kOutput, calls=%fused_computation.56 | convolution fusion | flops 1610612736 | bytes 15073280 | tf_op jit(solution)/shard_map/dot_general | solution.py:116
  (41 shorter events, 3.7 us)
Async XLA Ops:
  1.3 6.7 %copy-start.5 = (s32[768,12]{0,1:T(8,128)S(1)}, s32[768,12]{0,1:T(8,128)}, u32[]{:S(2)}) copy-start(s32[768,12]{0,1:T(8,128)} %param.7) | copy-start | bytes 110596
  2.8 510.7 %collective-permute-start = (bf16[2,640,128]{2,1,0:T(8,128)(2,1)S(1)}, bf16[2,640,128]{2,1,0:T(8,128)(2,1)S(1)}, u32[]{:S(2)}, u32[]{:S(2)}) collective-permute-start(bf16[2,640,128]{2,1,0:T(8,128)(2,1)S(1)} %get-tuple-element.26), channel_id=1, source_target_pairs={{0,4},{4,8},{8,12},{1,5},{5,9},{9,13},{2,6},{6,10},{10,14},{3,7},{... | collective-permute-start | bytes 983048 | tf_op jit(solution)/shard_map/ppermute | solution.py:19
  6.8 506.7 %collective-permute-start.1 = (bf16[2,640,128]{2,1,0:T(8,128)(2,1)S(1)}, bf16[2,640,128]{2,1,0:T(8,128)(2,1)S(1)}, u32[]{:S(2)}, u32[]{:S(2)}) collective-permute-start(bf16[2,640,128]{2,1,0:T(8,128)(2,1)S(1)} %get-tuple-element.27), channel_id=1, source_target_pairs={{4,0},{8,4},{12,8},{5,1},{9,5},{13,9},{6,2},{10,6},{14,10},{7,3},{... | collective-permute-start | bytes 983048 | tf_op jit(solution)/shard_map/ppermute | solution.py:22
  15.9 530.3 %all-to-all-start = ((s32[64,1,128]{2,1,0:T(1,128)}), s32[64,1,128]{2,1,0:T(1,128)}, u32[]{:S(2)}, u32[]{:S(2)}) async-start(s32[64,1,128]{2,1,0:T(1,128)} %bitcast.49), calls=%async_computation | async-start | bytes 65536 | tf_op jit(solution)/shard_map/all_to_all | solution.py:101
  28.7 0.7 copy-start.7
  513.6 8.1 %collective-permute-start.2 = (bf16[2,10,512]{2,1,0:T(8,128)(2,1)S(1)}, bf16[2,10,512]{2,1,0:T(8,128)(2,1)S(1)}, u32[]{:S(2)}, u32[]{:S(2)}) collective-permute-start(bf16[2,10,512]{2,1,0:T(8,128)(2,1)S(1)} %get-tuple-element.24), channel_id=1, source_target_pairs={{0,1},{1,2},{2,3},{4,5},{5,6},{6,7},{8,9},{9,10},{10,11},{12,13},{... | collective-permute-start | bytes 61448 | tf_op jit(solution)/shard_map/ppermute | solution.py:19
  516.9 4.8 collective-permute-start.3
  529.3 1.9 copy-start.3
  531.2 1.3 copy-start.2
  532.5 1.3 copy-start.1
  533.9 1.3 copy-start
  543.9 1.7 copy-start.4
  556.4 11.7 %copy-start.6 = (s32[72,128]{1,0:T(8,128)S(1)}, s32[72,128]{1,0:T(8,128)}, u32[]{:S(2)}) copy-start(s32[72,128]{1,0:T(8,128)} %get-tuple-element.28) | copy-start | bytes 110596
  556.4 61.6 %all-to-all-start.1 = ((bf16[64,128,128]{2,1,0:T(8,128)(2,1)}), bf16[64,128,128]{2,1,0:T(8,128)(2,1)S(1)}, u32[]{:S(2)}, u32[]{:S(2)}) async-start(bf16[64,128,128]{2,1,0:T(8,128)(2,1)} %fusion.28), calls=%async_computation.1 | async-start | bytes 4194304 | tf_op jit(solution)/shard_map/all_to_all | solution.py:106
where the time goes:
time: 631 us; the launch traced here: 628 us
  local copies, waits for them, and re-layouts  497 us (79%)
  matrix products  59.2 us (9%)
  starting transfers between devices  34.5 us (5%)
  waiting for transfers between devices  27.7 us (4%)
  other arithmetic  9.34 us (1%)
    gather x2, local copies, waits for them, and re-layouts, shards(): kernel[:, tap_clipped]  484 us
    all_to_all x1, waiting for transfers between devices, shards(): lax.all_to_all(outgoing, ('apa', 'band'), split_axis=0, concat_axis=0, ti...  27.7 us
    dot_general x1, matrix products, shards(): jnp.einsum('bkg,bks->bgs', source_hot.reshape(blob_count, places, groups)...  21.2 us
    all_to_all x1, starting transfers between devices, shards(): lax.all_to_all(request, ('apa', 'band'), split_axis=0, concat_axis=0, til...  12.8 us
  transfers between devices with their start and end apart: 6, of which 1 were waited for; matrix products, arithmetic and copies ran while one was open for 86% of the time, Pallas kernels for 0%

commit v1 on v0

--- a/solution.py
+++ b/solution.py
@@ -3,6 +3,8 @@
 import jax
 import jax.numpy as jnp
 from jax import lax
+from jax.experimental import pallas as pl
+from jax.experimental.pallas import tpu as pltpu
 from jax.sharding import PartitionSpec as P
 
 W = 2560
@@ -49,18 +51,44 @@
     return (inside + offsets[:, None, :]).reshape(entries, groups)
 
 
+def tap_tables(kernel):
+    offsets = 2 * WR + 1
+    size = 2 * H
+
+    def body(k_ref, out_ref, k32):
+        k32[0:offsets, 0 : size + 1] = k_ref[...].astype(jnp.float32)
+        source = lax.broadcasted_iota(jnp.int32, (size, size), 0)
+        target = lax.broadcasted_iota(jnp.int32, (size, size), 1)
+
+        def one(p, carry):
+            row = k32[pl.ds(p, 1), 0:size]
+            last = k32[pl.ds(p, 1), size : 2 * size][:, 0:1]
+            taps = pltpu.roll(jnp.broadcast_to(row, (size, size)), 0, 1, stride=1, stride_axis=0)
+            low = jnp.where(target < source, taps, jnp.where(target == source, last, 0.0))
+            out_ref[p, 0:size, :] = low.astype(jnp.bfloat16)
+            out_ref[p, size : 2 * size, :] = jnp.where(target >= source, taps, 0.0).astype(jnp.bfloat16)
+            return carry
+
+        lax.fori_loop(0, offsets, one, 0)
+
+    return pl.pallas_call(
+        body,
+        out_shape=jax.ShapeDtypeStruct((offsets, 2 * size, size), jnp.bfloat16),
+        in_specs=[pl.BlockSpec(memory_space=pltpu.VMEM)],
+        out_specs=pl.BlockSpec(memory_space=pltpu.VMEM),
+        scratch_shapes=[pltpu.VMEM((24, 2 * size), jnp.float32)],
+        compiler_params=pltpu.CompilerParams(vmem_limit_bytes=24 << 20),
+        cost_estimate=pl.CostEstimate(flops=0, bytes_accessed=6 << 20, transcendentals=0),
+    )(kernel)
+
+
 def shards(raw, dead_mask, kernel, blob_wires):
     apa_count, band_wires, slab_ticks = raw.shape
     length = slab_ticks + 2 * H
     clean = raw * dead_mask.astype(jnp.bfloat16)[:, :, None]
     extended = with_halo(clean, (("slab", 2),), H)
     widened = with_halo(extended, (("band", 1),), WR)
-    source_tick = jnp.arange(length, dtype=jnp.int32)
-    target_tick = jnp.arange(slab_ticks, dtype=jnp.int32)
-    tap_place = target_tick[None, :] - source_tick[:, None] + 2 * H
-    valid_tap = (tap_place >= 0) & (tap_place <= 2 * H)
-    tap_clipped = jnp.clip(tap_place, 0, 2 * H)
-    tables = jnp.where(valid_tap[None, :, :], kernel[:, tap_clipped], jnp.zeros((), jnp.bfloat16))
+    tables = tap_tables(kernel)
     total = jnp.zeros((apa_count * band_wires, slab_ticks), jnp.float32)
     for offset in range(2 * WR + 1):
         shifted = widened[:, offset : offset + band_wires].reshape(apa_count * band_wires, length)

time: 631 us -> 150 us (0.24)
  local copies, waits for them, and re-layouts: 497 us -> 13.2 us
    gather x2 -> x0, local copies, waits for them, and re-layouts: 484 us -> none  [shards(): kernel[:, tap_clipped]]
  transfers between devices with their start and end apart: 6 -> 6, of which waited for: 1 -> 3; matrix products, arithmetic and copies ran while one was open for 86% -> 34% of each run, Pallas kernels for 0% -> 2%
where the time goes in v1:
time: 150 us; the launch traced here: 149 us
  matrix products  58.4 us (39%)
  starting transfers between devices  34.9 us (23%)
  waiting for transfers between devices  33.2 us (22%)
  local copies, waits for them, and re-layouts  13.2 us (9%)
  other arithmetic  5.19 us (3%)
  Pallas kernels  3.14 us (2%)
    all_to_all x1, waiting for transfers between devices, shards(): lax.all_to_all(outgoing, ('apa', 'band'), split_axis=0, concat_axis=0, ti...  27.7 us
    dot_general x1, matrix products, shards(): jnp.einsum('bkg,bks->bgs', source_hot.reshape(blob_count, places, groups)...  21.3 us
    all_to_all x1, starting transfers between devices, shards(): lax.all_to_all(request, ('apa', 'band'), split_axis=0, concat_axis=0, til...  14.9 us
    dot_general x21, matrix products, shards(): jnp.dot(shifted, tables[offset], preferred_element_type=jnp.float32)  12 us
    dot_general x1, matrix products, shards(): jnp.dot(placement, incoming, preferred_element_type=jnp.float32)  10.4 us
    all_to_all x1, starting transfers between devices, shards(): lax.all_to_all(outgoing, ('apa', 'band'), split_axis=0, concat_axis=0, ti...  10.3 us
    dot_general x1, matrix products, shards(): jnp.einsum('gsr,rt->gst', pick_table, slice_rows, preferred_element_type=...  9.35 us
    ppermute x2, starting transfers between devices, with_halo(): lax.ppermute(lax.slice_in_dim(block, block.shape[dim] - width, None, axis...  7.15 us
  transfers between devices with their start and end apart: 6, of which 3 were waited for; matrix products, arithmetic and copies ran while one was open for 34% of the time, Pallas kernels for 2%

profile of v1, /device:TPU:1, one launch (start us, length us, event | category | flops | bytes accessed | tf_op | source)
XLA Modules:
  0.0 149.1 jit_solution(6237310053621233628)
XLA Ops:
  0.6 0.7 convert_element_type.59
  1.3 1.3 broadcast_multiply_fusion
  2.8 4.0 %collective-permute-start = (bf16[2,640,128]{2,1,0:T(8,128)(2,1)S(1)}, bf16[2,640,128]{2,1,0:T(8,128)(2,1)S(1)}, u32[]{:S(2)}, u32[]{:S(2)}) collective-permute-start(bf16[2,640,128]{2,1,0:T(8,128)(2,1)S(1)} %get-tuple-element.26), channel_id=1, source_target_pairs={{0,4},{4,8},{8,12},{1,5},{5,9},{9,13},{2,6},{6,10},{10,14},{3,7},{... | collective-permute-start | bytes 983048 | tf_op jit(solution)/shard_map/ppermute | solution.py:21
  6.8 1.3 collective-permute-start.1
  9.1 0.9 convert_reduce_fusion
  10.1 1.3 fusion.17
  11.4 1.7 %collective-permute-done = bf16[2,640,128]{2,1,0:T(8,128)(2,1)S(1)} collective-permute-done((bf16[2,640,128]{2,1,0:T(8,128)(2,1)S(1)}, bf16[2,640,128]{2,1,0:T(8,128)(2,1)S(1)}, u32[]{:S(2)}, u32[]{:S(2)}) %collective-permute-start) | collective-permute-done | bytes 327712 | tf_op jit(solution)/shard_map/ppermute | solution.py:21
  13.1 3.8 %collective-permute-done.1 = bf16[2,640,128]{2,1,0:T(8,128)(2,1)S(1)} collective-permute-done((bf16[2,640,128]{2,1,0:T(8,128)(2,1)S(1)}, bf16[2,640,128]{2,1,0:T(8,128)(2,1)S(1)}, u32[]{:S(2)}, u32[]{:S(2)}) %collective-permute-start.1) | collective-permute-done | bytes 327712 | tf_op jit(solution)/shard_map/ppermute | solution.py:24
  17.1 0.5 copy-done.8
  17.6 3.2 %collective-permute-start.2 = (bf16[2,10,512]{2,1,0:T(8,128)(2,1)S(1)}, bf16[2,10,512]{2,1,0:T(8,128)(2,1)S(1)}, u32[]{:S(2)}, u32[]{:S(2)}) collective-permute-start(bf16[2,10,512]{2,1,0:T(8,128)(2,1)S(1)} %get-tuple-element.24), channel_id=1, source_target_pairs={{0,1},{1,2},{2,3},{4,5},{5,6},{6,7},{8,9},{9,10},{10,11},{12,13},{... | collective-permute-start | bytes 61448 | tf_op jit(solution)/shard_map/ppermute | solution.py:21
  20.8 1.3 collective-permute-start.3
  22.1 3.9 %fusion.43 = s32[64,128]{1,0:T(8,128)} fusion(s32[9216]{0:T(1024)S(1)} %get-tuple-element.29, pred[9216]{0:T(1024)(128)(4,1)S(1)} %broadcast_compare_fusion.1, f32[9216]{0:T(1024)S(1)} %get-tuple-element.31, s32[9216]{0:T(1024)S(1)} %get-tuple-element.30), kind=kOutput, calls=%fused_computation.61 | convolution fusion | flops 910114816 | bytes 152576 | tf_op jit(solution)/shard_map/dot_general | solution.py:122
  26.0 14.9 %all-to-all-start = ((s32[64,1,128]{2,1,0:T(1,128)}), s32[64,1,128]{2,1,0:T(1,128)S(1)}, u32[]{:S(2)}, u32[]{:S(2)}) async-start(s32[64,1,128]{2,1,0:T(1,128)} %bitcast.47), calls=%async_computation | async-start | bytes 65536 | tf_op jit(solution)/shard_map/all_to_all | solution.py:129
  41.0 3.1 %shard_map.59 = bf16[21,512,256]{2,1,0:T(8,128)(2,1)S(1)} custom-call(bf16[21,257]{1,0:T(8,128)(2,1)S(1)} %copy-done), custom_call_target="tpu_custom_call" | custom-call | bytes 6291456 | tf_op jit(solution)/shard_map/pallas_call | solution.py:74
  44.1 0.6 maximum_maximum_fusion
  44.7 3.6 %fusion.77 = (bf16[2,640,512]{2,1,0:T(8,128)(2,1)S(1)}, bf16[2,640,512]{2,1,0:T(8,128)(2,1)S(1)}, bf16[2,640,512]{2,1,0:T(8,128)(2,1)S(1)}, bf16[2,640,512]{2,1,...) fusion(bf16[2,650,512]{2,1,0:T(8,128)(2,1)S(1)} %get-tuple-elem, ...), kind=kLoop, calls=%fused_computation.156 | loop fusion | bytes 26214400 | tf_op jit(solution)/shard_map/slice | solution.py:94
  48.4 3.4 %fusion.76 = (bf16[2,640,512]{2,1,0:T(8,128)(2,1)S(1)}, bf16[2,640,512]{2,1,0:T(8,128)(2,1)S(1)}, bf16[2,640,512]{2,1,0:T(8,128)(2,1)S(1)}, bf16[2,640,512]{2,1,...) fusion(bf16[2,650,512]{2,1,0:T(8,128)(2,1)S(1)} %get-tuple-elem, ...), kind=kLoop, calls=%fused_computation.155 | loop fusion | bytes 26214400 | tf_op jit(solution)/shard_map/slice | solution.py:94
  51.8 1.9 %fusion.49 = f32[1280,256]{1,0:T(8,128)S(1)} fusion(bf16[1280,512]{1,0:T(8,128)(2,1)} %bitcast.148, bf16[21,512,256]{2,1,0:T(8,128)(2,1)S(1)} %shard_map.59), kind=kOutput, calls=%fused_computation.84 | convolution fusion | flops 335544320 | bytes 2883584 | tf_op jit(solution)/shard_map/dot_general | solution.py:95
  53.7 0.5 fusion.48
  54.2 0.8 copy-done.3
  55.0 0.5 convolution_add_fusion.18
  55.5 0.8 copy-done.2
  56.4 0.5 convolution_add_fusion.17
  56.9 0.8 copy-done.1
  57.7 0.5 convolution_add_fusion.16
  58.2 0.5 convolution_add_fusion.15
  58.7 0.5 convolution_add_fusion.14
  59.2 0.5 convolution_add_fusion.13
  59.7 0.5 convolution_add_fusion.12
  60.2 0.5 convolution_add_fusion.11
  60.7 0.5 convolution_add_fusion.10
  61.2 0.5 fusion.15
  61.8 0.5 convolution_add_fusion.8
  62.3 0.5 convolution_add_fusion.7
  62.8 0.5 convolution_add_fusion.6
  63.3 0.5 convolution_add_fusion.5
  63.8 0.5 convolution_add_fusion.4
  64.3 0.5 convolution_add_fusion.3
  64.9 0.5 convolution_add_fusion.2
  65.4 0.5 convolution_add_fusion.1
  65.9 0.5 fusion.16
  67.2 1.2 reduce_sum.32
  68.5 0.7 copy.39
  69.2 9.3 %fusion.28 = bf16[64,128,128]{2,1,0:T(8,128)(2,1)} fusion(bf16[1280,128,1]{1,0,2:T(8,128)(2,1)S(1)} %bitcast.151, s32[64,128]{1,0:T(8,128)S(1)} %bitcast.152), kind=kOutput, calls=%fused_computation.49 | convolution fusion | flops 2695888896 | bytes 2457600 | tf_op jit(solution)/shard_map/gsr,rt->gst/dot_general | solution.py:132
  78.5 10.3 %all-to-all-start.1 = ((bf16[64,128,128]{2,1,0:T(8,128)(2,1)}), bf16[64,128,128]{2,1,0:T(8,128)(2,1)S(1)}, u32[]{:S(2)}, u32[]{:S(2)}) async-start(bf16[64,128,128]{2,1,0:T(8,128)(2,1)} %fusion.28), calls=%async_computation.1 | async-start | bytes 4194304 | tf_op jit(solution)/shard_map/all_to_all | solution.py:134
  89.8 21.3 %convolution_convert_fusion = bf16[768,64,128]{2,1,0:T(8,128)(2,1)} fusion(s32[768,12]{1,0:T(8,128)S(1)} %convert_element_type.64, s32[768,12]{1,0:T(8,128)S(1)} %copy.27, pred[768,12]{1,0:T(8,128)(4,1)S(1)} %copy.28), kind=kOutput, calls=%fused_computation.5 | convolution fusion | flops 160825344 | bytes 12665856 | tf_op jit(solution)/shard_map/bkg,bks->bgs/dot_general | solution.py:136
  111.0 27.7 %all-to-all-done.1 = bf16[64,128,128]{2,1,0:T(8,128)(2,1)S(1)} async-done(((bf16[64,128,128]{2,1,0:T(8,128)(2,1)}), bf16[64,128,128]{2,1,0:T(8,128)(2,1)S(1)}, u32[]{:S(2)}, u32[]{:S(2)}) %all-to-all-start.1) | async-done | bytes 2097184 | tf_op jit(solution)/shard_map/all_to_all | solution.py:134
  138.7 10.4 %fusion.29 = f32[768,128]{1,0:T(8,128)} fusion(bf16[64,128,128]{2,1,0:T(8,128)(2,1)S(1)} %all-to-all-done.1, bf16[768,64,128]{2,1,0:T(8,128)(2,1)} %convolution_convert_fusion), kind=kOutput, calls=%fused_computation.53 | convolution fusion | flops 1610612736 | bytes 15073280 | tf_op jit(solution)/shard_map/dot_general | solution.py:144
  (40 shorter events, 3.2 us)
Async XLA Ops:
  1.3 6.7 %copy-start.10 = (s32[768,12]{0,1:T(8,128)S(1)}, s32[768,12]{0,1:T(8,128)}, u32[]{:S(2)}) copy-start(s32[768,12]{0,1:T(8,128)} %param.7) | copy-start | bytes 110596
  2.8 10.3 %collective-permute-start = (bf16[2,640,128]{2,1,0:T(8,128)(2,1)S(1)}, bf16[2,640,128]{2,1,0:T(8,128)(2,1)S(1)}, u32[]{:S(2)}, u32[]{:S(2)}) collective-permute-start(bf16[2,640,128]{2,1,0:T(8,128)(2,1)S(1)} %get-tuple-element.26), channel_id=1, source_target_pairs={{0,4},{4,8},{8,12},{1,5},{5,9},{9,13},{2,6},{6,10},{10,14},{3,7},{... | collective-permute-start | bytes 983048 | tf_op jit(solution)/shard_map/ppermute | solution.py:21
  6.8 10.2 %collective-permute-start.1 = (bf16[2,640,128]{2,1,0:T(8,128)(2,1)S(1)}, bf16[2,640,128]{2,1,0:T(8,128)(2,1)S(1)}, u32[]{:S(2)}, u32[]{:S(2)}) collective-permute-start(bf16[2,640,128]{2,1,0:T(8,128)(2,1)S(1)} %get-tuple-element.27), channel_id=1, source_target_pairs={{4,0},{8,4},{12,8},{5,1},{9,5},{13,9},{6,2},{10,6},{14,10},{7,3},{... | collective-permute-start | bytes 983048 | tf_op jit(solution)/shard_map/ppermute | solution.py:24
  13.1 4.0 %copy-start.6 = (bf16[2,640,128]{2,1,0:T(8,128)(2,1)}, bf16[2,640,128]{2,1,0:T(8,128)(2,1)S(1)}, u32[]{:S(2)}) copy-start(bf16[2,640,128]{2,1,0:T(8,128)(2,1)S(1)} %collective-permute-done) | copy-start | bytes 983044
  16.9 0.7 copy-start.8
  17.6 26.5 %collective-permute-start.2 = (bf16[2,10,512]{2,1,0:T(8,128)(2,1)S(1)}, bf16[2,10,512]{2,1,0:T(8,128)(2,1)S(1)}, u32[]{:S(2)}, u32[]{:S(2)}) collective-permute-start(bf16[2,10,512]{2,1,0:T(8,128)(2,1)S(1)} %get-tuple-element.24), channel_id=1, source_target_pairs={{0,1},{1,2},{2,3},{4,5},{5,6},{6,7},{8,9},{9,10},{10,11},{12,13},{... | collective-permute-start | bytes 61448 | tf_op jit(solution)/shard_map/ppermute | solution.py:21
  20.8 23.3 %collective-permute-start.3 = (bf16[2,10,512]{2,1,0:T(8,128)(2,1)S(1)}, bf16[2,10,512]{2,1,0:T(8,128)(2,1)S(1)}, u32[]{:S(2)}, u32[]{:S(2)}) collective-permute-start(bf16[2,10,512]{2,1,0:T(8,128)(2,1)S(1)} %get-tuple-element.25), channel_id=1, source_target_pairs={{1,0},{2,1},{3,2},{5,4},{6,5},{7,6},{9,8},{10,9},{11,10},{13,12},{... | collective-permute-start | bytes 61448 | tf_op jit(solution)/shard_map/ppermute | solution.py:24
  22.1 18.8 %copy-start = (bf16[21,257]{1,0:T(8,128)(2,1)S(1)}, bf16[21,257]{1,0:T(8,128)(2,1)}, u32[]{:S(2)}) copy-start(bf16[21,257]{1,0:T(8,128)(2,1)} %k_ref.1) | copy-start | bytes 32386
  26.0 43.1 %all-to-all-start = ((s32[64,1,128]{2,1,0:T(1,128)}), s32[64,1,128]{2,1,0:T(1,128)S(1)}, u32[]{:S(2)}, u32[]{:S(2)}) async-start(s32[64,1,128]{2,1,0:T(1,128)} %bitcast.47), calls=%async_computation | async-start | bytes 65536 | tf_op jit(solution)/shard_map/all_to_all | solution.py:129
  40.9 3.2 %copy-start.7 = (bf16[2,640,128]{2,1,0:T(8,128)(2,1)S(1)}, bf16[2,640,128]{2,1,0:T(8,128)(2,1)}, u32[]{:S(2)}) copy-start(bf16[2,640,128]{2,1,0:T(8,128)(2,1)} %copy-done.6) | copy-start | bytes 983044
  40.9 3.2 %copy-start.9 = (bf16[2,640,128]{2,1,0:T(8,128)(2,1)S(1)}, bf16[2,640,128]{2,1,0:T(8,128)(2,1)}, u32[]{:S(2)}) copy-start(bf16[2,640,128]{2,1,0:T(8,128)(2,1)} %copy-done.8) | copy-start | bytes 983044
  51.8 1.9 %copy-start.4 = (bf16[2,640,512]{2,1,0:T(8,128)(2,1)S(1)}, bf16[2,640,512]{2,1,0:T(8,128)(2,1)}, u32[]{:S(2)}) copy-start(bf16[2,640,512]{2,1,0:T(8,128)(2,1)} %get-tuple-element.11) | copy-start | bytes 3932164
  53.7 1.3 copy-start.3
  55.0 1.3 copy-start.2
  56.4 1.3 copy-start.1
  66.4 0.8 copy-start.5
  78.5 60.2 %all-to-all-start.1 = ((bf16[64,128,128]{2,1,0:T(8,128)(2,1)}), bf16[64,128,128]{2,1,0:T(8,128)(2,1)S(1)}, u32[]{:S(2)}, u32[]{:S(2)}) async-start(bf16[64,128,128]{2,1,0:T(8,128)(2,1)} %fusion.28), calls=%async_computation.1 | async-start | bytes 4194304 | tf_op jit(solution)/shard_map/all_to_all | solution.py:134

commit v2 on v0

v2 whole, which is shorter than its diff:
```python
import jax
import jax.numpy as jnp
from jax import lax
from jax.experimental import pallas as pl
from jax.experimental.pallas import tpu as pltpu
from jax.sharding import PartitionSpec as P

W = 2560
WR = 10
H = 128
TAPS = 2 * WR + 1
BANDS = 4
SLABS = 4
PLANES = 8
PEERS = 8
WIRES = W // BANDS
TICKS = 2 * H
LONG = 2 * TICKS
EDGE = 16
TALL = WIRES + 2 * EDGE
SLICES = TICKS // 2
SLOTS = 128
BLOBS = 768
PLACES = 12
COLS = 40
LANES = 128
BF = jnp.bfloat16
F32 = jnp.float32
MESH = pl.DeviceIdType.MESH


def iota(shape, dim):
    return lax.broadcasted_iota(jnp.int32, shape, dim)


def dot(a, b):
    return jnp.dot(a, b, preferred_element_type=F32)


def build_tables(k_ref, k32, tab):
    k32[...] = jnp.zeros_like(k32)
    k32[0:TAPS, 0 : TICKS + 1] = k_ref[...].astype(F32)
    source = iota((TICKS, TICKS), 0)
    target = iota((TICKS, TICKS), 1)

    def one(p, carry):
        row = k32[pl.ds(p, 1), 0:TICKS]
        last = k32[pl.ds(p, 1), TICKS:LONG][:, 0:1]
        taps = pltpu.roll(jnp.broadcast_to(row, (TICKS, TICKS)), 0, 1, stride=1, stride_axis=0)
        low = jnp.where(target < source, taps, jnp.where(target == source, last, 0.0))
        tab[p, 0:TICKS, :] = low.astype(BF)
        tab[p, TICKS:LONG, :] = jnp.where(target >= source, taps, 0.0).astype(BF)
        return carry

    lax.fori_loop(0, TAPS, one, 0)


def mask_waves(raw_ref, mask_ref, mask8, clean):
    mask8[...] = jnp.zeros_like(mask8)
    mask8[0:2, :] = mask_ref[...].astype(F32)
    live = jnp.transpose(mask8[...])
    for ap in range(2):
        wave = raw_ref[ap].astype(F32) * live[:, ap : ap + 1]
        clean[ap, EDGE : EDGE + WIRES, H : H + TICKS] = wave.astype(BF)


def interleave(clean, xf, xi, ap, has):
    left, right, above, below = has
    rows = ((0, EDGE, above), (EDGE, EDGE + WIRES, None), (EDGE + WIRES, TALL, below))
    cols = ((0, H, left), (H, H + TICKS, None), (H + TICKS, LONG, right))
    for r0, r1, row_ok in rows:
        for c0, c1, col_ok in cols:
            part = clean[ap, r0:r1, c0:c1].astype(F32)
            if row_ok is not None:
                part = jnp.where(row_ok, part, 0.0)
            if col_ok is not None:
                part = jnp.where(col_ok, part, 0.0)
            for t in range((c1 - c0) // LANES):
                xf[c0 // LANES + t, r0:r1, :] = part[:, t * LANES : (t + 1) * LANES]
    first = EDGE - WR

    def one(i, carry):
        for t in range(LONG // LANES):
            picked = xf[t, pl.ds(i + first, 16, stride=COLS), :]
            xi[ap, i, :, t * LANES : (t + 1) * LANES] = picked.astype(BF)
        return carry

    lax.fori_loop(0, COLS + 2 * WR, one, 0, unroll=4)


def convolve(xi, tab, so, sig_v, held, pair_sum, ap):
    tile = 20
    group = 7

    def one(n, carry):
        i0 = n * tile
        total = None
        for g in range(TAPS // group):
            parts = [
                xi[ap, pl.ds(i0 + g * group + q, tile)].reshape(tile * 16, LONG) for q in range(group)
            ]
            lhs = jnp.concatenate(parts, axis=1)
            rhs = tab[g * group : (g + 1) * group].reshape(group * LONG, TICKS)
            term = dot(lhs, rhs)
            total = term if total is None else total + term
        for i in range(tile):
            for t in range(TICKS // LANES):
                so[t, pl.ds(i0 + i, 16, stride=COLS), :] = total[
                    16 * i : 16 * (i + 1), t * LANES : (t + 1) * LANES
                ]
        return carry

    lax.fori_loop(0, COLS // tile, one, 0)
    wave = jnp.concatenate([so[t] for t in range(TICKS // LANES)], axis=1).astype(BF)
    sig_v[ap] = wave
    held[0, ap * WIRES : (ap + 1) * WIRES, :] = dot(wave, pair_sum).astype(BF)


def make_requests(wires_ref, request, bslot, packed, lower):
    refs = wires_ref[...]
    usable = refs >= 0
    wire = jnp.where(usable, refs, 0)
    apa = ((wire >> 9) * 205) >> 10
    wire = wire - apa * W
    band = ((wire >> 7) * 205) >> 10
    row = (apa & 1) * WIRES + wire - band * WIRES
    source = jnp.where(usable, (apa >> 1) * BANDS + band, 255)
    packed[...] = jnp.zeros_like(packed)
    packed[:, 0:PLACES] = source.astype(F32)
    packed[:, 16 : 16 + PLACES] = ((row >> 7) + 1).astype(F32)
    packed[:, 32 : 32 + PLACES] = (row & 127).astype(F32)
    entries = packed[...].astype(BF)
    spread_row = iota((LANES, 2 * LANES), 0)
    spread_col = iota((LANES, 2 * LANES), 1)
    base = jnp.where(spread_col < LANES, 0, jnp.where(spread_col < 192, 16, 32))
    lane = iota((BLOBS, LANES), 1)
    group_of = (lane & 63).astype(F32)
    slot_of = lane.astype(F32)
    blob = iota((BLOBS, LANES), 0)
    blob_value = jnp.where(lane < 64, (blob >> 7) + 1, blob & 127).astype(F32)
    block = BLOBS // 3
    lower[...] = (iota((block, block), 0) > iota((block, block), 1)).astype(F32).astype(BF)
    ones_top = (iota((LANES, LANES), 0) < 64).astype(F32).astype(BF)

    def one(k, carry):
        offset, total = carry
        spread = (spread_row == base + k).astype(F32).astype(BF)
        wide = dot(entries, spread)
        hot = (wide[:, 0:LANES] == group_of).astype(F32)
        hot16 = hot.astype(BF)
        ranks = []
        for j in range(3):
            piece = hot16[j * block : (j + 1) * block]
            inside = dot(lower[...], piece)
            ranks.append(inside + offset)
            offset = offset + inside[block - 1 : block] + hot[(j + 1) * block - 1 : (j + 1) * block]
        rank = jnp.concatenate(ranks, axis=0)
        slot = dot((hot * rank).astype(BF), ones_top)
        slot_hot = (slot == slot_of).astype(F32).astype(BF)
        values = jnp.concatenate(
            [(hot * wide[:, LANES:]).astype(BF), (hot * blob_value).astype(BF)], axis=1
        )
        found = lax.dot_general(
            slot_hot, values, (((0,), (0,)), ((), ())), preferred_element_type=F32
        )
        return offset, total + found

    _, table = lax.fori_loop(
        0, PLACES, one, (jnp.zeros((1, LANES), F32), jnp.zeros((SLOTS, 2 * LANES), F32))
    )
    request[...] = table[:, 0:LANES].astype(BF)
    high = table[:, LANES:]
    low = pltpu.roll(high, 64, 1)
    bslot[...] = jnp.transpose(high * 128.0 - 128.0 + low)


def pick(reqbox, held, picks, slot, plane, core, band):
    group = plane * 8 + core * BANDS + band
    place = iota((LANES, LANES), 0)
    choose = jnp.where(place == group, 128.0, jnp.where(place == group + 64, 1.0, 0.0)).astype(BF)
    lane = iota((2 * SLOTS, LANES), 1).astype(F32)

    def one(n, carry):
        asked = reqbox[pl.ds(2 * n, 2)].reshape(2 * SLOTS, LANES)
        row = dot(asked, choose)
        tiles = [
            (row == lane + 128.0 * (t + 1)).astype(F32).astype(BF) for t in range(2 * WIRES // LANES)
        ]
        got = dot(jnp.concatenate(tiles, axis=1), held[slot])
        picks[slot, pl.ds(2 * n, 2)] = got.astype(BF).reshape(2, SLOTS, SLICES)
        return carry

    lax.fori_loop(0, PEERS // 2, one, 0)


def place(bslot, picks, inbox, total, slot, plane, core, band):
    rows = []
    blocks = []
    for r in range(PEERS):
        dc, dy = divmod(r, BANDS)
        from_core = lax.rem(core + dc, 2)
        from_band = lax.rem(band + BANDS - dy, BANDS)
        rows.append(bslot[pl.ds(plane * 8 + from_core * BANDS + from_band, 1), :])
        blocks.append(picks[slot, 0] if r == 0 else inbox[slot, r])
    incoming = jnp.concatenate(blocks, axis=0)
    tile = 256
    blob = iota((tile, LANES), 0)

    def one(n, carry):
        index = (blob + n * tile).astype(F32)
        hot = jnp.concatenate([(index == row).astype(F32).astype(BF) for row in rows], axis=1)
        at = pl.ds(pl.multiple_of(n * tile, tile), tile)
        total[at, :] = total[at, :] + dot(hot, incoming)
        return carry

    lax.fori_loop(0, BLOBS // tile, one, 0)


def whole(
    raw_ref, mask_ref, k_ref, wires_ref, sig_ref, blob_ref,
    clean, xf, xi, tab, k32, mask8, so, sig_v, held, packed, lower, request, bslot,
    reqbox, picks, inbox,
    halo_send, halo_recv, req_send, req_recv, ring_send, ring_recv, box_send, box_recv, out_sem,
):
    apa = lax.axis_index("apa")
    slab = lax.axis_index("slab")
    band = lax.axis_index("band")
    plane = lax.div(apa, 2)
    core = lax.rem(apa, 2)

    def device(dz=0, dc=0, dx=0, dy=0):
        z = lax.rem(plane + dz + PLANES, PLANES)
        c = lax.rem(core + dc, 2)
        return (z * 2 + c, lax.rem(slab + dx + SLABS, SLABS), lax.rem(band + dy + BANDS, BANDS))

    peers = [device(dc=r // BANDS, dy=r % BANDS) for r in range(PEERS)]
    everyone = peers[1:] + [device(dz=1), device(dz=-1), device(dx=1), device(dx=-1)]
    everyone += [device(dx=i, dy=j) for i in (-1, 1) for j in (-1, 1)]
    barrier = pltpu.get_barrier_semaphore()
    for other in everyone:
        pl.semaphore_signal(barrier, inc=1, device_id=other, device_id_type=MESH)

    mask_waves(raw_ref, mask_ref, mask8, clean)
    pl.semaphore_wait(barrier, len(everyone))

    def remote(src, dst, send, recv, to):
        return pltpu.make_async_remote_copy(
            src_ref=src, dst_ref=dst, send_sem=send, recv_sem=recv, device_id=to, device_id_type=MESH
        )

    own = slice(EDGE, EDGE + WIRES)
    mid = slice(H, H + TICKS)
    row_parts = {
        -1: (slice(EDGE, 2 * EDGE), slice(EDGE + WIRES, TALL)),
        0: (own, own),
        1: (slice(WIRES, EDGE + WIRES), slice(0, EDGE)),
    }
    col_parts = {
        -1: (slice(H, 2 * H), slice(H + TICKS, LONG)),
        0: (mid, mid),
        1: (slice(2 * H, 3 * H), slice(0, H)),
    }
    halos = {0: [], 1: []}
    number = 0
    for ap in range(2):
        for dx in (-1, 0, 1):
            for dy in (-1, 0, 1):
                if dx == 0 and dy == 0:
                    continue
                (rs, rd), (cs, cd) = row_parts[dy], col_parts[dx]
                copy = remote(
                    clean.at[ap, rs, cs], clean.at[ap, rd, cd],
                    halo_send.at[number], halo_recv.at[number], device(dx=dx, dy=dy),
                )
                copy.start()
                halos[ap].append(copy)
                number += 1

    make_requests(wires_ref, request, bslot, packed, lower)
    reqbox[0] = request[...]
    asks = []
    for r in range(1, PEERS):
        dc, dy = divmod(r, BANDS)
        back = dc * BANDS + (BANDS - dy) % BANDS
        copy = remote(request, reqbox.at[back], req_send.at[back], req_recv.at[back], peers[r])
        copy.start()
        asks.append(copy)

    build_tables(k_ref, k32, tab)
    pair_sum = (iota((TICKS, SLICES), 0) >> 1) == iota((TICKS, SLICES), 1)
    pair_sum = pair_sum.astype(F32).astype(BF)
    has = (slab > 0, slab < SLABS - 1, band > 0, band < BANDS - 1)

    def half(ap):
        return slice(ap * WIRES, (ap + 1) * WIRES)

    towards = (device(dz=1), device(dz=-1))

    def slot_at(way, distance):
        if distance == 0:
            return 0
        if distance == 4:
            return 7
        return distance + 3 * way

    def ring(way, distance, ap):
        number = 2 * (distance - 1) + (ap if distance < 4 else 0)
        return remote(
            held.at[slot_at(way, distance - 1), half(ap)],
            held.at[slot_at(way, distance), half(ap)],
            ring_send.at[way, number], ring_recv.at[way, number], towards[way],
        )

    writes = []
    started = []
    for ap in range(2):
        for copy in halos[ap]:
            copy.wait_recv()
        interleave(clean, xf, xi, ap, has)
        convolve(xi, tab, so, sig_v, held, pair_sum, ap)
        for way in range(2):
            copy = ring(way, 1, ap)
            copy.start()
            started.append(copy)
        write = pltpu.make_async_copy(sig_v.at[ap], sig_ref.at[ap], out_sem.at[ap])
        write.start()
        writes.append(write)

    blob_ref[...] = jnp.zeros_like(blob_ref)
    for copy in asks:
        copy.wait_recv()
    boxes = {}

    def serve(slot, shift):
        source = lax.rem(plane + shift + PLANES, PLANES)
        pick(reqbox, held, picks, slot, source, core, band)
        boxes[slot] = []
        for r in range(1, PEERS):
            copy = remote(
                picks.at[slot, r], inbox.at[slot, r], box_send.at[slot, r], box_recv.at[slot, r], peers[r]
            )
            copy.start()
            boxes[slot].append(copy)

    def collect(slot, shift):
        source = lax.rem(plane + shift + PLANES, PLANES)
        for copy in boxes[slot]:
            copy.wait_recv()
        place(bslot, picks, inbox, blob_ref, slot, source, core, band)

    def forward(distance, ap):
        for way in range(2):
            ring(way, distance, ap).wait_recv()
            if distance < 3 or ap == way:
                copy = ring(way, distance + 1, ap)
                copy.start()
                started.append(copy)

    serve(0, 0)
    forward(1, 0)
    collect(0, 0)
    forward(1, 1)
    serve(1, -1)
    forward(2, 0)
    serve(4, 1)
    collect(1, -1)
    forward(2, 1)
    serve(2, -2)
    collect(4, 1)
    forward(3, 0)
    serve(5, 2)
    collect(2, -2)
    forward(3, 1)
    serve(3, -3)
    serve(6, 3)
    collect(5, 2)
    collect(3, -3)
    ring(0, 4, 0).wait_recv()
    ring(1, 4, 1).wait_recv()
    serve(7, 4)
    collect(6, 3)
    collect(7, 4)

    for copies in (halos[0], halos[1], asks, started, *boxes.values()):
        for copy in copies:
            copy.wait_send()
    for write in writes:
        write.wait()


def shards(raw, dead_mask, kernel, blob_wires):
    vmem = pl.BlockSpec(memory_space=pltpu.VMEM)
    dma = pltpu.SemaphoreType.DMA
    return pl.pallas_call(
        whole,
        out_shape=(
            jax.ShapeDtypeStruct((2, WIRES, TICKS), BF),
            jax.ShapeDtypeStruct((BLOBS, SLICES), F32),
        ),
        in_specs=[vmem] * 4,
        out_specs=(pl.BlockSpec(memory_space=pl.ANY), vmem),
        scratch_shapes=[
            pltpu.VMEM((2, TALL, LONG), BF),
            pltpu.VMEM((LONG // LANES, TALL, LANES), F32),
            pltpu.VMEM((2, COLS + 2 * WR, 16, LONG), BF),
            pltpu.VMEM((TAPS, LONG, TICKS), BF),
            pltpu.VMEM((24, LONG), F32),
            pltpu.VMEM((8, WIRES), F32),
            pltpu.VMEM((TICKS // LANES, WIRES, LANES), F32),
            pltpu.VMEM((2, WIRES, TICKS), BF),
            pltpu.VMEM((PLANES, 2 * WIRES, SLICES), BF),
            pltpu.VMEM((BLOBS, LANES), F32),
            pltpu.VMEM((BLOBS // 3, BLOBS // 3), BF),
            pltpu.VMEM((SLOTS, LANES), BF),
            pltpu.VMEM((LANES, SLOTS), F32),
            pltpu.VMEM((PEERS, SLOTS, LANES), BF),
            pltpu.VMEM((PLANES, PEERS, SLOTS, SLICES), BF),
            pltpu.VMEM((PLANES, PEERS, SLOTS, SLICES), BF),
            dma((16,)),
            dma((16,)),
            dma((PEERS,)),
            dma((PEERS,)),
            dma((2, 7)),
            dma((2, 7)),
            dma((PLANES, PEERS)),
            dma((PLANES, PEERS)),
            dma((2,)),
        ],
        compiler_params=pltpu.CompilerParams(
            collective_id=0, has_side_effects=True, vmem_limit_bytes=56 << 20
        ),
    )(raw, dead_mask, kernel, blob_wires)


def solution(mesh):
    return jax.shard_map(
        shards,
        mesh=mesh,
        in_specs=(P("apa", "band", "slab"), P("apa", "band"), P(), P(("apa", "band"), None)),
        out_specs=(P("apa", "band", "slab"), P(("apa", "band"), "slab")),
        check_vma=False,
    )
```

time: 631 us -> 82.9 us (0.13)
  local copies, waits for them, and re-layouts: 497 us -> 4.49 us
  Pallas kernels: 0 us -> 77.2 us
  matrix products: 59.2 us -> 0 us
  starting transfers between devices: 34.5 us -> 0 us
  waiting for transfers between devices: 27.7 us -> 0 us
  other arithmetic: 9.34 us -> 0 us
    gather x2 -> x0, local copies, waits for them, and re-layouts: 484 us -> none  [shards(): kernel[:, tap_clipped]]
    pallas_call x0 -> x1, Pallas kernels: none -> 77.2 us  [shards(): pl.pallas_call(whole, out_shape=(jax.ShapeDtypeStruct((2, WIRES, TICKS),...]
    dot_general x27 -> x0, matrix products: 59.2 us -> none  [the longest x1 21.2 us: shards(): jnp.einsum('bkg,bks->bgs', source_hot.reshape(blob_count, places, groups)...]
    all_to_all x2 -> x0, waiting for transfers between devices: 27.7 us -> none  [the longest x1 27.7 us: shards(): lax.all_to_all(outgoing, ('apa', 'band'), split_axis=0, concat_axis=0, ti...]
    all_to_all x2 -> x0, starting transfers between devices: 24.5 us -> none  [the longest x1 12.8 us: shards(): lax.all_to_all(request, ('apa', 'band'), split_axis=0, concat_axis=0, til...]
    ppermute x4 -> x0, starting transfers between devices: 10 us -> none  [the longest x2 7.25 us: with_halo(): lax.ppermute(lax.slice_in_dim(block, block.shape[dim] - width, None, axis...]
    slice x4 -> x0, local copies, waits for them, and re-layouts: 7.12 us -> none  [the longest x2 6.99 us: shards(): widened[:, offset:offset + band_wires]]
  transfers between devices with their start and end apart: 6 -> 0, of which waited for: 1 -> 0; matrix products, arithmetic and copies ran while one was open for 86% -> 0% of each run, Pallas kernels for 0% -> 0%
where the time goes in v2:
time: 82.9 us; the launch traced here: 82.3 us
  Pallas kernels  77.2 us (93%)
  local copies, waits for them, and re-layouts  4.49 us (5%)
    pallas_call x1, Pallas kernels, shards(): pl.pallas_call(whole, out_shape=(jax.ShapeDtypeStruct((2, WIRES, TICKS),...  77.2 us
    unnamed x5, local copies, waits for them, and re-layouts  4.49 us

profile of v2, /device:TPU:1, one launch (start us, length us, event | category | flops | bytes accessed | tf_op | source)
XLA Modules:
  0.0 82.3 jit_solution(8983955158686963350)
XLA Ops:
  0.6 1.7 %copy.6.wires_ref = s32[768,12]{1,0:T(8,128)} copy(s32[768,12]{0,1:T(8,128)} %param.7) | data formatting | bytes 73728 | tf_op args[3]
  2.4 77.2 %shard_map.59 = (bf16[2,640,256]{2,1,0:T(8,128)(2,1)}, f32[768,128]{1,0:T(8,128)}) custom-call(bf16[2,640,256]{2,1,0:T(8,128)(2,1)} %raw_ref.1, s32[2,640]{1,0:T(2,128)} %mask_ref.1, bf16[21,257]{1,0:T(8,128)(2,1)} %k_ref.1, s32[768,12]{1,0:T(8,128)} %copy.6.wires_ref), custom_call_target="tpu_custom_call" | custom-call | tf_op jit(solution)/shard_map/pallas_call | solution.py:394
  79.5 0.0 copy-start
  79.5 2.0 %copy.9 = bf16[2,640,256]{2,1,0:T(8,128)(2,1)} copy(bf16[2,640,256]{2,1,0:T(8,128)(2,1)} %get-tuple-element.4) | data formatting | bytes 1310720
  81.6 0.0 copy-done
  81.6 0.7 copy.10
Async XLA Ops:
  79.5 2.0 %copy-start = (f32[768,128]{1,0:T(8,128)S(1)}, f32[768,128]{1,0:T(8,128)}, u32[]{:S(2)}) copy-start(f32[768,128]{1,0:T(8,128)} %get-tuple-element.5) | copy-start | bytes 1179652

commit v3 on v2

--- a/solution.py
+++ b/solution.py
@@ -16,6 +16,7 @@
 WIRES = W // BANDS
 TICKS = 2 * H
 LONG = 2 * TICKS
+REACH = 3 * H
 EDGE = 16
 TALL = WIRES + 2 * EDGE
 SLICES = TICKS // 2
@@ -24,6 +25,9 @@
 PLACES = 12
 COLS = 40
 LANES = 128
+GROUPS = 64
+PICK_OWNERS = 8
+CONV_GROUPS = tuple((u, u + 2) for u in range(0, 22, 2))
 BF = jnp.bfloat16
 F32 = jnp.float32
 MESH = pl.DeviceIdType.MESH
@@ -40,16 +44,23 @@
 def build_tables(k_ref, k32, tab):
     k32[...] = jnp.zeros_like(k32)
     k32[0:TAPS, 0 : TICKS + 1] = k_ref[...].astype(F32)
-    source = iota((TICKS, TICKS), 0)
-    target = iota((TICKS, TICKS), 1)
+    source = iota((H, H), 0)
+    target = iota((H, H), 1)
+    nothing = jnp.zeros((REACH, H), BF)
+    tab[0, :, H:TICKS] = nothing
+    tab[TAPS, :, 0:H] = nothing
 
     def one(p, carry):
         row = k32[pl.ds(p, 1), 0:TICKS]
         last = k32[pl.ds(p, 1), TICKS:LONG][:, 0:1]
         taps = pltpu.roll(jnp.broadcast_to(row, (TICKS, TICKS)), 0, 1, stride=1, stride_axis=0)
-        low = jnp.where(target < source, taps, jnp.where(target == source, last, 0.0))
-        tab[p, 0:TICKS, :] = low.astype(BF)
-        tab[p, TICKS:LONG, :] = jnp.where(target >= source, taps, 0.0).astype(BF)
+        near = taps[0:H, 0:H]
+        first = jnp.where(source > target, near, jnp.where(target == source, last, 0.0)).astype(BF)
+        second = taps[H:TICKS, 0:H].astype(BF)
+        third = jnp.where(target >= source, near, 0.0).astype(BF)
+        for n, part in enumerate((first, second, third)):
+            tab[p, n * H : (n + 1) * H, 0:H] = part
+            tab[p + 1, n * H : (n + 1) * H, H:TICKS] = part
         return carry
 
     lax.fori_loop(0, TAPS, one, 0)
@@ -82,41 +93,46 @@
     def one(i, carry):
         for t in range(LONG // LANES):
             picked = xf[t, pl.ds(i + first, 16, stride=COLS), :]
-            xi[ap, i, :, t * LANES : (t + 1) * LANES] = picked.astype(BF)
+            xi[ap, lax.div(i, 2), lax.rem(i, 2), :, t * LANES : (t + 1) * LANES] = picked.astype(BF)
         return carry
 
     lax.fori_loop(0, COLS + 2 * WR, one, 0, unroll=4)
 
 
 def convolve(xi, tab, so, sig_v, held, pair_sum, ap):
-    tile = 20
-    group = 7
-
-    def one(n, carry):
-        i0 = n * tile
+    pairs = COLS // 2
+    for tb in range(TICKS // H):
         total = None
-        for g in range(TAPS // group):
+        for u0, u1 in CONV_GROUPS:
             parts = [
-                xi[ap, pl.ds(i0 + g * group + q, tile)].reshape(tile * 16, LONG) for q in range(group)
+                xi[ap, u // 2 : u // 2 + pairs, u % 2, :, tb * H : tb * H + REACH].reshape(
+                    pairs * 16, REACH
+                )
+                for u in range(u0, u1)
             ]
-            lhs = jnp.concatenate(parts, axis=1)
-            rhs = tab[g * group : (g + 1) * group].reshape(group * LONG, TICKS)
-            term = dot(lhs, rhs)
+            rhs = tab[u0:u1].reshape((u1 - u0) * REACH, TICKS)
+            term = dot(jnp.concatenate(parts, axis=1), rhs)
             total = term if total is None else total + term
-        for i in range(tile):
-            for t in range(TICKS // LANES):
-                so[t, pl.ds(i0 + i, 16, stride=COLS), :] = total[
-                    16 * i : 16 * (i + 1), t * LANES : (t + 1) * LANES
+        for i in range(pairs):
+            for n in range(2):
+                so[tb, pl.ds(2 * i + n, 16, stride=COLS), :] = total[
+                    16 * i : 16 * (i + 1), n * H : (n + 1) * H
                 ]
-        return carry
-
-    lax.fori_loop(0, COLS // tile, one, 0)
     wave = jnp.concatenate([so[t] for t in range(TICKS // LANES)], axis=1).astype(BF)
     sig_v[ap] = wave
     held[0, ap * WIRES : (ap + 1) * WIRES, :] = dot(wave, pair_sum).astype(BF)
 
 
-def make_requests(wires_ref, request, bslot, packed, lower):
+def tall(row, height):
+    block = jnp.broadcast_to(row, (16, row.shape[1])).astype(BF)
+    return jnp.concatenate([block] * (height // 16), axis=0)
+
+
+def one_if(hit):
+    return jnp.where(hit, jnp.ones((), BF), jnp.zeros((), BF))
+
+
+def make_requests(wires_ref, request, bslot, hots, counts, upper):
     refs = wires_ref[...]
     usable = refs >= 0
     wire = jnp.where(usable, refs, 0)
@@ -124,101 +140,105 @@
     wire = wire - apa * W
     band = ((wire >> 7) * 205) >> 10
     row = (apa & 1) * WIRES + wire - band * WIRES
-    source = jnp.where(usable, (apa >> 1) * BANDS + band, 255)
-    packed[...] = jnp.zeros_like(packed)
-    packed[:, 0:PLACES] = source.astype(F32)
-    packed[:, 16 : 16 + PLACES] = ((row >> 7) + 1).astype(F32)
-    packed[:, 32 : 32 + PLACES] = (row & 127).astype(F32)
-    entries = packed[...].astype(BF)
-    spread_row = iota((LANES, 2 * LANES), 0)
-    spread_col = iota((LANES, 2 * LANES), 1)
-    base = jnp.where(spread_col < LANES, 0, jnp.where(spread_col < 192, 16, 32))
-    lane = iota((BLOBS, LANES), 1)
-    group_of = (lane & 63).astype(F32)
-    slot_of = lane.astype(F32)
-    blob = iota((BLOBS, LANES), 0)
-    blob_value = jnp.where(lane < 64, (blob >> 7) + 1, blob & 127).astype(F32)
+    source = jnp.where(usable, (apa >> 1) * BANDS + band, 255).astype(F32)
+    row_high = ((row >> 7) + 1).astype(F32)
+    row_low = (row & 127).astype(F32)
+    blob = iota((1, BLOBS), 1)
+    blob_high = tall(((blob >> 7) + 1).astype(F32), GROUPS)
+    blob_low = tall((blob & 127).astype(F32), GROUPS)
     block = BLOBS // 3
-    lower[...] = (iota((block, block), 0) > iota((block, block), 1)).astype(F32).astype(BF)
-    ones_top = (iota((LANES, LANES), 0) < 64).astype(F32).astype(BF)
-
-    def one(k, carry):
-        offset, total = carry
-        spread = (spread_row == base + k).astype(F32).astype(BF)
-        wide = dot(entries, spread)
-        hot = (wide[:, 0:LANES] == group_of).astype(F32)
-        hot16 = hot.astype(BF)
-        ranks = []
-        for j in range(3):
-            piece = hot16[j * block : (j + 1) * block]
-            inside = dot(lower[...], piece)
-            ranks.append(inside + offset)
-            offset = offset + inside[block - 1 : block] + hot[(j + 1) * block - 1 : (j + 1) * block]
-        rank = jnp.concatenate(ranks, axis=0)
-        slot = dot((hot * rank).astype(BF), ones_top)
-        slot_hot = (slot == slot_of).astype(F32).astype(BF)
+    upper[0 : 2 * block, :] = jnp.ones((2 * block, block), BF)
+    upper[2 * block :, :] = (
+        (iota((block, block), 0) < iota((block, block), 1)).astype(F32).astype(BF)
+    )
+    group = iota((GROUPS, BLOBS), 0).astype(F32).astype(BF)
+    slot = iota((SLOTS, BLOBS), 0).astype(F32).astype(BF)
+    for k in range(PLACES):
+        hots[k * GROUPS : (k + 1) * GROUPS, :] = one_if(group == tall(source[k : k + 1], GROUPS))
+    for j in range(3):
+        counts[:, j * block : (j + 1) * block] = dot(
+            hots[:, 0 : (j + 1) * block], upper[(2 - j) * block :, :]
+        )
+    before = jnp.zeros((GROUPS, 1), F32)
+    table = jnp.zeros((4 * GROUPS, SLOTS), F32)
+    for k in range(PLACES):
+        here = slice(k * GROUPS, (k + 1) * GROUPS)
+        hot = hots[here, :]
+        hot32 = hot.astype(F32)
+        count = counts[here, :]
+        rank = jnp.sum(hot32 * (count + before), axis=0, keepdims=True)
+        before = before + (count + hot32)[:, BLOBS - 1 : BLOBS]
+        slot_hot = one_if(slot == tall(rank, SLOTS))
         values = jnp.concatenate(
-            [(hot * wide[:, LANES:]).astype(BF), (hot * blob_value).astype(BF)], axis=1
+            [
+                hot * tall(row_high[k : k + 1], GROUPS),
+                hot * tall(row_low[k : k + 1], GROUPS),
+                hot * blob_high,
+                hot * blob_low,
+            ],
+            axis=0,
         )
-        found = lax.dot_general(
-            slot_hot, values, (((0,), (0,)), ((), ())), preferred_element_type=F32
+        table = table + lax.dot_general(
+            values, slot_hot, (((1,), (1,)), ((), ())), preferred_element_type=F32
         )
-        return offset, total + found
-
-    _, table = lax.fori_loop(
-        0, PLACES, one, (jnp.zeros((1, LANES), F32), jnp.zeros((SLOTS, 2 * LANES), F32))
-    )
-    request[...] = table[:, 0:LANES].astype(BF)
-    high = table[:, LANES:]
-    low = pltpu.roll(high, 64, 1)
-    bslot[...] = jnp.transpose(high * 128.0 - 128.0 + low)
+    request[...] = jnp.transpose(table[0 : 2 * GROUPS]).astype(BF)
+    bslot[...] = table[2 * GROUPS :]
 
 
 def pick(reqbox, held, picks, slot, plane, core, band):
     group = plane * 8 + core * BANDS + band
-    place = iota((LANES, LANES), 0)
-    choose = jnp.where(place == group, 128.0, jnp.where(place == group + 64, 1.0, 0.0)).astype(BF)
-    lane = iota((2 * SLOTS, LANES), 1).astype(F32)
+    index = iota((LANES, 2 * LANES), 0)
+    choose = index == jnp.where(iota((LANES, 2 * LANES), 1) < LANES, group, group + GROUPS)
+    choose = choose.astype(F32).astype(BF)
+    height = PICK_OWNERS * SLOTS
+    lane = iota((height, LANES), 1).astype(F32).astype(BF)
 
     def one(n, carry):
-        asked = reqbox[pl.ds(2 * n, 2)].reshape(2 * SLOTS, LANES)
-        row = dot(asked, choose)
+        at = pl.ds(PICK_OWNERS * n, PICK_OWNERS)
+        asked = reqbox[at].reshape(height, LANES)
+        wide = dot(asked, choose)
+        high = wide[:, 0:LANES].astype(BF)
+        low = one_if(wide[:, LANES:].astype(BF) == lane)
         tiles = [
-            (row == lane + 128.0 * (t + 1)).astype(F32).astype(BF) for t in range(2 * WIRES // LANES)
+            jnp.where(high == jnp.asarray(t + 1, BF), low, jnp.zeros((), BF))
+            for t in range(2 * WIRES // LANES)
         ]
         got = dot(jnp.concatenate(tiles, axis=1), held[slot])
-        picks[slot, pl.ds(2 * n, 2)] = got.astype(BF).reshape(2, SLOTS, SLICES)
+        picks[slot, at] = got.astype(BF).reshape(PICK_OWNERS, SLOTS, SLICES)
         return carry
 
-    lax.fori_loop(0, PEERS // 2, one, 0)
+    lax.fori_loop(0, PEERS // PICK_OWNERS, one, 0)
 
 
 def place(bslot, picks, inbox, total, slot, plane, core, band):
-    rows = []
+    highs = []
+    lows = []
     blocks = []
+    blob = iota((SLOTS, LANES), 0).astype(F32).astype(BF)
     for r in range(PEERS):
         dc, dy = divmod(r, BANDS)
         from_core = lax.rem(core + dc, 2)
         from_band = lax.rem(band + BANDS - dy, BANDS)
-        rows.append(bslot[pl.ds(plane * 8 + from_core * BANDS + from_band, 1), :])
+        group = plane * 8 + from_core * BANDS + from_band
+        highs.append(tall(bslot[pl.ds(group, 1), :], SLOTS))
+        lows.append(one_if(blob == tall(bslot[pl.ds(group + GROUPS, 1), :], SLOTS)))
         blocks.append(picks[slot, 0] if r == 0 else inbox[slot, r])
     incoming = jnp.concatenate(blocks, axis=0)
-    tile = 256
-    blob = iota((tile, LANES), 0)
-
-    def one(n, carry):
-        index = (blob + n * tile).astype(F32)
-        hot = jnp.concatenate([(index == row).astype(F32).astype(BF) for row in rows], axis=1)
-        at = pl.ds(pl.multiple_of(n * tile, tile), tile)
-        total[at, :] = total[at, :] + dot(hot, incoming)
-        return carry
-
-    lax.fori_loop(0, BLOBS // tile, one, 0)
+    high = jnp.concatenate(highs, axis=1)
+    low = jnp.concatenate(lows, axis=1)
+    hot = jnp.concatenate(
+        [
+            jnp.where(high == jnp.asarray(m + 1, BF), low, jnp.zeros((), BF))
+            for m in range(BLOBS // LANES)
+        ],
+        axis=0,
+    )
+    total[...] = total[...] + dot(hot, incoming)
 
 
 def whole(
     raw_ref, mask_ref, k_ref, wires_ref, sig_ref, blob_ref,
-    clean, xf, xi, tab, k32, mask8, so, sig_v, held, packed, lower, request, bslot,
+    clean, xf, xi, tab, k32, mask8, so, sig_v, held, hots, counts, upper, request, bslot,
     reqbox, picks, inbox,
     halo_send, halo_recv, req_send, req_recv, ring_send, ring_recv, box_send, box_recv, out_sem,
 ):
@@ -276,7 +296,7 @@
                 halos[ap].append(copy)
                 number += 1
 
-    make_requests(wires_ref, request, bslot, packed, lower)
+    make_requests(wires_ref, request, bslot, hots, counts, upper)
     reqbox[0] = request[...]
     asks = []
     for r in range(1, PEERS):
@@ -402,15 +422,16 @@
         scratch_shapes=[
             pltpu.VMEM((2, TALL, LONG), BF),
             pltpu.VMEM((LONG // LANES, TALL, LANES), F32),
-            pltpu.VMEM((2, COLS + 2 * WR, 16, LONG), BF),
-            pltpu.VMEM((TAPS, LONG, TICKS), BF),
+            pltpu.VMEM((2, COLS // 2 + WR, 2, 16, LONG), BF),
+            pltpu.VMEM((TAPS + 1, REACH, TICKS), BF),
             pltpu.VMEM((24, LONG), F32),
             pltpu.VMEM((8, WIRES), F32),
             pltpu.VMEM((TICKS // LANES, WIRES, LANES), F32),
             pltpu.VMEM((2, WIRES, TICKS), BF),
             pltpu.VMEM((PLANES, 2 * WIRES, SLICES), BF),
-            pltpu.VMEM((BLOBS, LANES), F32),
-            pltpu.VMEM((BLOBS // 3, BLOBS // 3), BF),
+            pltpu.VMEM((PLACES * GROUPS, BLOBS), BF),
+            pltpu.VMEM((PLACES * GROUPS, BLOBS), F32),
+            pltpu.VMEM((BLOBS, BLOBS // 3), BF),
             pltpu.VMEM((SLOTS, LANES), BF),
             pltpu.VMEM((LANES, SLOTS), F32),
             pltpu.VMEM((PEERS, SLOTS, LANES), BF),
@@ -429,7 +450,7 @@
         compiler_params=pltpu.CompilerParams(
             collective_id=0, has_side_effects=True, vmem_limit_bytes=56 << 20
         ),
-    )(raw, dead_mask, kernel, blob_wires)
+    )(raw, dead_mask, kernel, blob_wires.T)
 
 
 def solution(mesh):

time: 82.9 us -> 71.8 us (0.87)
  Pallas kernels: 77.2 us -> 68.3 us
  local copies, waits for them, and re-layouts: 4.49 us -> 2.77 us
    pallas_call x1, Pallas kernels: 77.2 us -> 68.3 us  [shards(): pl.pallas_call(whole, out_shape=(jax.ShapeDtypeStruct((2, WIRES, TICKS),...]
    unnamed x5 -> x4, local copies, waits for them, and re-layouts: 4.49 us -> 2.77 us
where the time goes in v3:
time: 71.8 us; the launch traced here: 71.7 us
  Pallas kernels  68.3 us (95%)
  local copies, waits for them, and re-layouts  2.77 us (4%)
    pallas_call x1, Pallas kernels, shards(): pl.pallas_call(whole, out_shape=(jax.ShapeDtypeStruct((2, WIRES, TICKS),...  68.3 us
    unnamed x4, local copies, waits for them, and re-layouts  2.77 us

profile of v3, /device:TPU:1, one launch (start us, length us, event | category | flops | bytes accessed | tf_op | source)
XLA Modules:
  0.0 71.7 jit_solution(14033887901796916150)
XLA Ops:
  0.6 68.3 %shard_map.59 = (bf16[2,640,256]{2,1,0:T(8,128)(2,1)}, f32[768,128]{1,0:T(8,128)}) custom-call(bf16[2,640,256]{2,1,0:T(8,128)(2,1)} %raw_ref.1, s32[2,640]{1,0:T(2,128)} %mask_ref.1, bf16[21,257]{1,0:T(8,128)(2,1)} %k_ref.1, s32[12,768]{1,0:T(8,128)} %bitcast.1), custom_call_target="tpu_custom_call" | custom-call | tf_op jit(solution)/shard_map/pallas_call | solution.py:414
  68.9 0.0 copy-start
  68.9 2.0 %copy.8 = bf16[2,640,256]{2,1,0:T(8,128)(2,1)} copy(bf16[2,640,256]{2,1,0:T(8,128)(2,1)} %get-tuple-element.4) | data formatting | bytes 1310720
  70.9 0.0 copy-done
  71.0 0.7 %copy.9 = f32[768,128]{1,0:T(8,128)} copy(f32[768,128]{1,0:T(8,128)S(1)} %copy-done) | data formatting | bytes 786432
Async XLA Ops:
  68.9 2.0 %copy-start = (f32[768,128]{1,0:T(8,128)S(1)}, f32[768,128]{1,0:T(8,128)}, u32[]{:S(2)}) copy-start(f32[768,128]{1,0:T(8,128)} %get-tuple-element.5) | copy-start | bytes 1179652

commit v4 on v3

--- a/solution.py
+++ b/solution.py
@@ -27,6 +27,7 @@
 LANES = 128
 GROUPS = 64
 PICK_OWNERS = 8
+PARTS = 2
 CONV_GROUPS = tuple((u, u + 2) for u in range(0, 22, 2))
 BF = jnp.bfloat16
 F32 = jnp.float32
@@ -52,23 +53,25 @@
 
     def one(p, carry):
         row = k32[pl.ds(p, 1), 0:TICKS]
+
+        def turned(start):
+            piece = jnp.broadcast_to(row[:, start : start + H], (H, H))
+            return pltpu.roll(piece, 0, 1, stride=1, stride_axis=0)
+
         last = k32[pl.ds(p, 1), TICKS:LONG][:, 0:1]
-        taps = pltpu.roll(jnp.broadcast_to(row, (TICKS, TICKS)), 0, 1, stride=1, stride_axis=0)
-        near = taps[0:H, 0:H]
-        first = jnp.where(source > target, near, jnp.where(target == source, last, 0.0)).astype(BF)
-        second = taps[H:TICKS, 0:H].astype(BF)
-        third = jnp.where(target >= source, near, 0.0).astype(BF)
+        early, late = turned(0), turned(H)
+        first = jnp.where(source > target, late, jnp.where(target == source, last, 0.0)).astype(BF)
+        second = jnp.where(target >= source, late, early).astype(BF)
+        third = jnp.where(target >= source, early, 0.0).astype(BF)
         for n, part in enumerate((first, second, third)):
             tab[p, n * H : (n + 1) * H, 0:H] = part
             tab[p + 1, n * H : (n + 1) * H, H:TICKS] = part
         return carry
 
-    lax.fori_loop(0, TAPS, one, 0)
-
-
-def mask_waves(raw_ref, mask_ref, mask8, clean):
-    mask8[...] = jnp.zeros_like(mask8)
-    mask8[0:2, :] = mask_ref[...].astype(F32)
+    lax.fori_loop(0, TAPS, one, 0, unroll=3)
+
+
+def mask_waves(raw_ref, mask8, clean):
     live = jnp.transpose(mask8[...])
     for ap in range(2):
         wave = raw_ref[ap].astype(F32) * live[:, ap : ap + 1]
@@ -93,34 +96,46 @@
     def one(i, carry):
         for t in range(LONG // LANES):
             picked = xf[t, pl.ds(i + first, 16, stride=COLS), :]
-            xi[ap, lax.div(i, 2), lax.rem(i, 2), :, t * LANES : (t + 1) * LANES] = picked.astype(BF)
+            picked = picked.astype(BF)
+            if t < 3:
+                xi[ap, lax.div(i, 2), lax.rem(i, 2), 0, :, t * LANES : (t + 1) * LANES] = picked
+            if t > 0:
+                xi[ap, lax.div(i, 2), lax.rem(i, 2), 1, :, (t - 1) * LANES : t * LANES] = picked
         return carry
 
     lax.fori_loop(0, COLS + 2 * WR, one, 0, unroll=4)
 
 
-def convolve(xi, tab, so, sig_v, held, pair_sum, ap):
-    pairs = COLS // 2
-    for tb in range(TICKS // H):
-        total = None
-        for u0, u1 in CONV_GROUPS:
-            parts = [
-                xi[ap, u // 2 : u // 2 + pairs, u % 2, :, tb * H : tb * H + REACH].reshape(
-                    pairs * 16, REACH
-                )
-                for u in range(u0, u1)
-            ]
-            rhs = tab[u0:u1].reshape((u1 - u0) * REACH, TICKS)
-            term = dot(jnp.concatenate(parts, axis=1), rhs)
-            total = term if total is None else total + term
-        for i in range(pairs):
-            for n in range(2):
-                so[tb, pl.ds(2 * i + n, 16, stride=COLS), :] = total[
-                    16 * i : 16 * (i + 1), n * H : (n + 1) * H
-                ]
-    wave = jnp.concatenate([so[t] for t in range(TICKS // LANES)], axis=1).astype(BF)
-    sig_v[ap] = wave
-    held[0, ap * WIRES : (ap + 1) * WIRES, :] = dot(wave, pair_sum).astype(BF)
+def convolve(xi, tab, so, waves, held, pair_sum, ap, part):
+    pairs = COLS // (2 * PARTS)
+    first = part * pairs
+    total = None
+    for u0, u1 in CONV_GROUPS:
+        pieces = [
+            xi[ap, first + u // 2 : first + u // 2 + pairs, u % 2].reshape(pairs * 32, REACH)
+            for u in range(u0, u1)
+        ]
+        rhs = tab[u0:u1].reshape((u1 - u0) * REACH, TICKS)
+        term = dot(jnp.concatenate(pieces, axis=1), rhs)
+        total = term if total is None else total + term
+    rows = pairs * 16
+    total = total.reshape(pairs, 2, 16, TICKS)
+    for n in range(2):
+        ends = [total[:, tb, :, n * H : (n + 1) * H].reshape(rows, H) for tb in range(2)]
+        for tb, end in enumerate(ends):
+            waves[n * rows : (n + 1) * rows, tb * H : (tb + 1) * H] = end.astype(BF)
+            for i in range(pairs):
+                wire = 2 * (first + i) + n
+                so[tb, pl.ds(wire, 16, stride=COLS), :] = end[16 * i : 16 * (i + 1)]
+    start = (ap * PARTS + part) * 2 * rows
+
+    def pairwise(n, carry):
+        at = pl.ds(pl.multiple_of(n * rows, rows), rows)
+        to = pl.ds(pl.multiple_of(start + n * rows, rows), rows)
+        held[0, to, :] = dot(waves[at, :], pair_sum[...]).astype(BF)
+        return carry
+
+    lax.fori_loop(0, 2, pairwise, 0)
 
 
 def tall(row, height):
@@ -139,7 +154,13 @@
     apa = ((wire >> 9) * 205) >> 10
     wire = wire - apa * W
     band = ((wire >> 7) * 205) >> 10
-    row = (apa & 1) * WIRES + wire - band * WIRES
+    wire = wire - band * WIRES
+    column = (wire * 1639) >> 16
+    wire = wire - column * COLS
+    pair = wire >> 1
+    part = jnp.where(pair >= COLS // 4, 1, 0)
+    row = (apa & 1) * WIRES + part * (WIRES // 2) + (wire & 1) * (WIRES // 4)
+    row = row + (pair - part * (COLS // 4)) * 16 + column
     source = jnp.where(usable, (apa >> 1) * BANDS + band, 255).astype(F32)
     row_high = ((row >> 7) + 1).astype(F32)
     row_low = (row & 127).astype(F32)
@@ -238,10 +259,12 @@
 
 def whole(
     raw_ref, mask_ref, k_ref, wires_ref, sig_ref, blob_ref,
-    clean, xf, xi, tab, k32, mask8, so, sig_v, held, hots, counts, upper, request, bslot,
+    clean, xf, xi, tab, k32, mask8, so, waves, pair_sum, sig_v, held, hots, counts, upper, request, bslot,
     reqbox, picks, inbox,
     halo_send, halo_recv, req_send, req_recv, ring_send, ring_recv, box_send, box_recv, out_sem,
 ):
+    fetch = pltpu.make_async_copy(raw_ref, sig_v, out_sem.at[2])
+    fetch.start()
     apa = lax.axis_index("apa")
     slab = lax.axis_index("slab")
     band = lax.axis_index("band")
@@ -260,7 +283,10 @@
     for other in everyone:
         pl.semaphore_signal(barrier, inc=1, device_id=other, device_id_type=MESH)
 
-    mask_waves(raw_ref, mask_ref, mask8, clean)
+    mask8[...] = jnp.zeros_like(mask8)
+    mask8[0:2, :] = mask_ref[...].astype(F32)
+    fetch.wait()
+    mask_waves(sig_v, mask8, clean)
     pl.semaphore_wait(barrier, len(everyone))
 
     def remote(src, dst, send, recv, to):
@@ -296,6 +322,9 @@
                 halos[ap].append(copy)
                 number += 1
 
+    build_tables(k_ref, k32, tab)
+    pair_hit = (iota((TICKS, SLICES), 0) >> 1) == iota((TICKS, SLICES), 1)
+    pair_sum[...] = pair_hit.astype(F32).astype(BF)
     make_requests(wires_ref, request, bslot, hots, counts, upper)
     reqbox[0] = request[...]
     asks = []
@@ -306,15 +335,10 @@
         copy.start()
         asks.append(copy)
 
-    build_tables(k_ref, k32, tab)
-    pair_sum = (iota((TICKS, SLICES), 0) >> 1) == iota((TICKS, SLICES), 1)
-    pair_sum = pair_sum.astype(F32).astype(BF)
     has = (slab > 0, slab < SLABS - 1, band > 0, band < BANDS - 1)
 
-    def half(ap):
-        return slice(ap * WIRES, (ap + 1) * WIRES)
-
     towards = (device(dz=1), device(dz=-1))
+    quarter = WIRES // PARTS
 
     def slot_at(way, distance):
         if distance == 0:
@@ -323,11 +347,15 @@
             return 7
         return distance + 3 * way
 
-    def ring(way, distance, ap):
-        number = 2 * (distance - 1) + (ap if distance < 4 else 0)
+    def ring(way, distance, piece):
+        if distance == 1:
+            number, rows = piece, slice(piece * quarter, (piece + 1) * quarter)
+        else:
+            number = 4 + 2 * (distance - 2) + (piece if distance < 4 else 0)
+            rows = slice(piece * WIRES, (piece + 1) * WIRES)
         return remote(
-            held.at[slot_at(way, distance - 1), half(ap)],
-            held.at[slot_at(way, distance), half(ap)],
+            held.at[slot_at(way, distance - 1), rows],
+            held.at[slot_at(way, distance), rows],
             ring_send.at[way, number], ring_recv.at[way, number], towards[way],
         )
 
@@ -337,18 +365,19 @@
         for copy in halos[ap]:
             copy.wait_recv()
         interleave(clean, xf, xi, ap, has)
-        convolve(xi, tab, so, sig_v, held, pair_sum, ap)
-        for way in range(2):
-            copy = ring(way, 1, ap)
-            copy.start()
-            started.append(copy)
+        for part in range(PARTS):
+            convolve(xi, tab, so.at[ap], waves, held, pair_sum, ap, part)
+            for way in range(2):
+                copy = ring(way, 1, ap * PARTS + part)
+                copy.start()
+                started.append(copy)
+
+    def write_signal(ap):
+        sig_v[ap] = jnp.concatenate([so[ap, t] for t in range(TICKS // LANES)], axis=1).astype(BF)
         write = pltpu.make_async_copy(sig_v.at[ap], sig_ref.at[ap], out_sem.at[ap])
         write.start()
         writes.append(write)
 
-    blob_ref[...] = jnp.zeros_like(blob_ref)
-    for copy in asks:
-        copy.wait_recv()
     boxes = {}
 
     def serve(slot, shift):
@@ -368,36 +397,45 @@
             copy.wait_recv()
         place(bslot, picks, inbox, blob_ref, slot, source, core, band)
 
-    def forward(distance, ap):
+    def forward(distance, half):
         for way in range(2):
-            ring(way, distance, ap).wait_recv()
-            if distance < 3 or ap == way:
-                copy = ring(way, distance + 1, ap)
+            if distance == 1:
+                for part in range(PARTS):
+                    ring(way, 1, half * PARTS + part).wait_recv()
+            else:
+                ring(way, distance, half).wait_recv()
+            if distance < 3 or half == way:
+                copy = ring(way, distance + 1, half)
                 copy.start()
                 started.append(copy)
 
+    forward(1, 0)
+    for copy in asks:
+        copy.wait_recv()
     serve(0, 0)
-    forward(1, 0)
-    collect(0, 0)
+    write_signal(0)
     forward(1, 1)
     serve(1, -1)
+    serve(4, 1)
+    write_signal(1)
+    blob_ref[...] = jnp.zeros_like(blob_ref)
     forward(2, 0)
-    serve(4, 1)
-    collect(1, -1)
+    collect(0, 0)
     forward(2, 1)
     serve(2, -2)
+    serve(5, 2)
+    collect(1, -1)
     collect(4, 1)
     forward(3, 0)
-    serve(5, 2)
-    collect(2, -2)
     forward(3, 1)
     serve(3, -3)
     serve(6, 3)
+    collect(2, -2)
     collect(5, 2)
-    collect(3, -3)
     ring(0, 4, 0).wait_recv()
     ring(1, 4, 1).wait_recv()
     serve(7, 4)
+    collect(3, -3)
     collect(6, 3)
     collect(7, 4)
 
@@ -408,25 +446,44 @@
         write.wait()
 
 
+def hand_over(signal, charge):
+    def body(signal_in, charge_in, signal_out, charge_out):
+        signal_out[...] = signal_in[...]
+        charge_out[...] = charge_in[...]
+
+    steps = 2
+    wave = pl.BlockSpec((2 // steps, WIRES, TICKS), lambda i: (i, 0, 0))
+    blob = pl.BlockSpec((BLOBS // steps, SLICES), lambda i: (i, 0))
+    return pl.pallas_call(
+        body,
+        grid=(steps,),
+        out_shape=tuple(jax.ShapeDtypeStruct(x.shape, x.dtype) for x in (signal, charge)),
+        in_specs=[wave, blob],
+        out_specs=(wave, blob),
+    )(signal, charge)
+
+
 def shards(raw, dead_mask, kernel, blob_wires):
     vmem = pl.BlockSpec(memory_space=pltpu.VMEM)
     dma = pltpu.SemaphoreType.DMA
-    return pl.pallas_call(
+    signal, charge = pl.pallas_call(
         whole,
         out_shape=(
             jax.ShapeDtypeStruct((2, WIRES, TICKS), BF),
             jax.ShapeDtypeStruct((BLOBS, SLICES), F32),
         ),
-        in_specs=[vmem] * 4,
+        in_specs=[pl.BlockSpec(memory_space=pl.ANY)] + [vmem] * 3,
         out_specs=(pl.BlockSpec(memory_space=pl.ANY), vmem),
         scratch_shapes=[
             pltpu.VMEM((2, TALL, LONG), BF),
             pltpu.VMEM((LONG // LANES, TALL, LANES), F32),
-            pltpu.VMEM((2, COLS // 2 + WR, 2, 16, LONG), BF),
+            pltpu.VMEM((2, COLS // 2 + WR, 2, 2, 16, REACH), BF),
             pltpu.VMEM((TAPS + 1, REACH, TICKS), BF),
             pltpu.VMEM((24, LONG), F32),
             pltpu.VMEM((8, WIRES), F32),
-            pltpu.VMEM((TICKS // LANES, WIRES, LANES), F32),
+            pltpu.VMEM((2, TICKS // LANES, WIRES, LANES), F32),
+            pltpu.VMEM((WIRES // PARTS, TICKS), BF),
+            pltpu.VMEM((TICKS, SLICES), BF),
             pltpu.VMEM((2, WIRES, TICKS), BF),
             pltpu.VMEM((PLANES, 2 * WIRES, SLICES), BF),
             pltpu.VMEM((PLACES * GROUPS, BLOBS), BF),
@@ -441,16 +498,17 @@
             dma((16,)),
             dma((PEERS,)),
             dma((PEERS,)),
-            dma((2, 7)),
-            dma((2, 7)),
+            dma((2, 9)),
+            dma((2, 9)),
             dma((PLANES, PEERS)),
             dma((PLANES, PEERS)),
-            dma((2,)),
+            dma((3,)),
         ],
         compiler_params=pltpu.CompilerParams(
             collective_id=0, has_side_effects=True, vmem_limit_bytes=56 << 20
         ),
     )(raw, dead_mask, kernel, blob_wires.T)
+    return hand_over(signal, charge)
 
 
 def solution(mesh):

time: 71.8 us -> 65.1 us (0.907)
  Pallas kernels: 68.3 us -> 64.3 us
  local copies, waits for them, and re-layouts: 2.77 us -> 0 us
    pallas_call x1, Pallas kernels: 68.3 us -> 62.2 us  [shards(): pl.pallas_call(whole, out_shape=(jax.ShapeDtypeStruct((2, WIRES, TICKS),...]
    unnamed x4 -> x0, local copies, waits for them, and re-layouts: 2.77 us -> none
    pallas_call x0 -> x1, Pallas kernels: none -> 2.06 us  [hand_over(): pl.pallas_call(body, grid=(steps,), out_shape=tuple((jax.ShapeDtypeStruct...]
where the time goes in v4:
time: 65.1 us; the launch traced here: 64.9 us
  Pallas kernels  64.3 us (99%)
    pallas_call x1, Pallas kernels, shards(): pl.pallas_call(whole, out_shape=(jax.ShapeDtypeStruct((2, WIRES, TICKS),...  62.2 us
    pallas_call x1, Pallas kernels, hand_over(): pl.pallas_call(body, grid=(steps,), out_shape=tuple((jax.ShapeDtypeStruct...  2.06 us

profile of v4, /device:TPU:1, one launch (start us, length us, event | category | flops | bytes accessed | tf_op | source)
XLA Modules:
  0.0 64.9 jit_solution(7420943480398250551)
XLA Ops:
  0.6 62.2 %shard_map.59 = (bf16[2,640,256]{2,1,0:T(8,128)(2,1)}, f32[768,128]{1,0:T(8,128)}) custom-call(bf16[2,640,256]{2,1,0:T(8,128)(2,1)} %raw_ref.1, s32[2,640]{1,0:T(2,128)} %mask_ref.1, bf16[21,257]{1,0:T(8,128)(2,1)} %k_ref.1, s32[12,768]{1,0:T(8,128)} %bitcast.1), custom_call_target="tpu_custom_call" | custom-call | tf_op jit(solution)/shard_map/pallas_call | solution.py:469
  62.9 2.1 %shard_map.60 = (bf16[2,640,256]{2,1,0:T(8,128)(2,1)}, f32[768,128]{1,0:T(8,128)}) custom-call(bf16[2,640,256]{2,1,0:T(8,128)(2,1)} %get-tuple-element.4.signal_in, f32[768,128]{1,0:T(8,128)} %get-tuple-element.5.charge_in), custom_call_target="tpu_custom_call" | custom-call | tf_op jit(solution)/shard_map/pallas_call | solution.py:457

commit v5 on v4

--- a/solution.py
+++ b/solution.py
@@ -68,14 +68,12 @@
             tab[p + 1, n * H : (n + 1) * H, H:TICKS] = part
         return carry
 
-    lax.fori_loop(0, TAPS, one, 0, unroll=3)
-
-
-def mask_waves(raw_ref, mask8, clean):
-    live = jnp.transpose(mask8[...])
-    for ap in range(2):
-        wave = raw_ref[ap].astype(F32) * live[:, ap : ap + 1]
-        clean[ap, EDGE : EDGE + WIRES, H : H + TICKS] = wave.astype(BF)
+    lax.fori_loop(0, TAPS, one, 0, unroll=TAPS)
+
+
+def mask_waves(raw, live, clean, ap):
+    wave = raw[ap].astype(F32) * live[:, ap : ap + 1]
+    clean[ap, EDGE : EDGE + WIRES, H : H + TICKS] = wave.astype(BF)
 
 
 def interleave(clean, xf, xi, ap, has):
@@ -103,7 +101,7 @@
                 xi[ap, lax.div(i, 2), lax.rem(i, 2), 1, :, (t - 1) * LANES : t * LANES] = picked
         return carry
 
-    lax.fori_loop(0, COLS + 2 * WR, one, 0, unroll=4)
+    lax.fori_loop(0, COLS + 2 * WR, one, 0, unroll=COLS + 2 * WR)
 
 
 def convolve(xi, tab, so, waves, held, pair_sum, ap, part):
@@ -147,7 +145,7 @@
     return jnp.where(hit, jnp.ones((), BF), jnp.zeros((), BF))
 
 
-def make_requests(wires_ref, request, bslot, hots, counts, upper):
+def count_places(wires_ref, fields, hots, counts, upper):
     refs = wires_ref[...]
     usable = refs >= 0
     wire = jnp.where(usable, refs, 0)
@@ -162,24 +160,27 @@
     row = (apa & 1) * WIRES + part * (WIRES // 2) + (wire & 1) * (WIRES // 4)
     row = row + (pair - part * (COLS // 4)) * 16 + column
     source = jnp.where(usable, (apa >> 1) * BANDS + band, 255).astype(F32)
-    row_high = ((row >> 7) + 1).astype(F32)
-    row_low = (row & 127).astype(F32)
-    blob = iota((1, BLOBS), 1)
-    blob_high = tall(((blob >> 7) + 1).astype(F32), GROUPS)
-    blob_low = tall((blob & 127).astype(F32), GROUPS)
+    fields[0:PLACES, :] = ((row >> 7) + 1).astype(F32)
+    fields[16 : 16 + PLACES, :] = (row & 127).astype(F32)
     block = BLOBS // 3
     upper[0 : 2 * block, :] = jnp.ones((2 * block, block), BF)
     upper[2 * block :, :] = (
         (iota((block, block), 0) < iota((block, block), 1)).astype(F32).astype(BF)
     )
     group = iota((GROUPS, BLOBS), 0).astype(F32).astype(BF)
-    slot = iota((SLOTS, BLOBS), 0).astype(F32).astype(BF)
     for k in range(PLACES):
         hots[k * GROUPS : (k + 1) * GROUPS, :] = one_if(group == tall(source[k : k + 1], GROUPS))
     for j in range(3):
         counts[:, j * block : (j + 1) * block] = dot(
             hots[:, 0 : (j + 1) * block], upper[(2 - j) * block :, :]
         )
+
+
+def make_requests(fields, request, bslot, hots, counts):
+    blob = iota((1, BLOBS), 1)
+    blob_high = tall(((blob >> 7) + 1).astype(F32), GROUPS)
+    blob_low = tall((blob & 127).astype(F32), GROUPS)
+    slot = iota((SLOTS, BLOBS), 0).astype(F32).astype(BF)
     before = jnp.zeros((GROUPS, 1), F32)
     table = jnp.zeros((4 * GROUPS, SLOTS), F32)
     for k in range(PLACES):
@@ -192,8 +193,8 @@
         slot_hot = one_if(slot == tall(rank, SLOTS))
         values = jnp.concatenate(
             [
-                hot * tall(row_high[k : k + 1], GROUPS),
-                hot * tall(row_low[k : k + 1], GROUPS),
+                hot * tall(fields[k : k + 1, :], GROUPS),
+                hot * tall(fields[16 + k : 17 + k, :], GROUPS),
                 hot * blob_high,
                 hot * blob_low,
             ],
@@ -259,12 +260,20 @@
 
 def whole(
     raw_ref, mask_ref, k_ref, wires_ref, sig_ref, blob_ref,
-    clean, xf, xi, tab, k32, mask8, so, waves, pair_sum, sig_v, held, hots, counts, upper, request, bslot,
+    mask_v, k_v, wires_v, clean, xf, xi, tab, k32, mask8, so, waves, pair_sum, sig_v, held, fields, hots, counts, upper, request, bslot,
     reqbox, picks, inbox,
     halo_send, halo_recv, req_send, req_recv, ring_send, ring_recv, box_send, box_recv, out_sem,
 ):
-    fetch = pltpu.make_async_copy(raw_ref, sig_v, out_sem.at[2])
-    fetch.start()
+    raw_v = sig_v
+    fetches = [
+        pltpu.make_async_copy(mask_ref, mask_v, out_sem.at[2]),
+        pltpu.make_async_copy(raw_ref.at[0], raw_v.at[0], out_sem.at[3]),
+        pltpu.make_async_copy(raw_ref.at[1], raw_v.at[1], out_sem.at[4]),
+        pltpu.make_async_copy(k_ref, k_v, out_sem.at[5]),
+        pltpu.make_async_copy(wires_ref, wires_v, out_sem.at[6]),
+    ]
+    for fetch in fetches:
+        fetch.start()
     apa = lax.axis_index("apa")
     slab = lax.axis_index("slab")
     band = lax.axis_index("band")
@@ -284,10 +293,9 @@
         pl.semaphore_signal(barrier, inc=1, device_id=other, device_id_type=MESH)
 
     mask8[...] = jnp.zeros_like(mask8)
-    mask8[0:2, :] = mask_ref[...].astype(F32)
-    fetch.wait()
-    mask_waves(sig_v, mask8, clean)
-    pl.semaphore_wait(barrier, len(everyone))
+    fetches[0].wait()
+    mask8[0:2, :] = mask_v[...].astype(F32)
+    live = jnp.transpose(mask8[...])
 
     def remote(src, dst, send, recv, to):
         return pltpu.make_async_remote_copy(
@@ -309,7 +317,13 @@
     halos = {0: [], 1: []}
     number = 0
     for ap in range(2):
-        for dx in (-1, 0, 1):
+        fetches[1 + ap].wait()
+        mask_waves(raw_v, live, clean, ap)
+        if ap == 0:
+            fetches[3].wait()
+            build_tables(k_v, k32, tab)
+            pl.semaphore_wait(barrier, len(everyone))
+        for dx in (-1, 1, 0):
             for dy in (-1, 0, 1):
                 if dx == 0 and dy == 0:
                     continue
@@ -322,10 +336,11 @@
                 halos[ap].append(copy)
                 number += 1
 
-    build_tables(k_ref, k32, tab)
     pair_hit = (iota((TICKS, SLICES), 0) >> 1) == iota((TICKS, SLICES), 1)
     pair_sum[...] = pair_hit.astype(F32).astype(BF)
-    make_requests(wires_ref, request, bslot, hots, counts, upper)
+    fetches[4].wait()
+    count_places(wires_v, fields, hots, counts, upper)
+    make_requests(fields, request, bslot, hots, counts)
     reqbox[0] = request[...]
     asks = []
     for r in range(1, PEERS):
@@ -334,7 +349,6 @@
         copy = remote(request, reqbox.at[back], req_send.at[back], req_recv.at[back], peers[r])
         copy.start()
         asks.append(copy)
-
     has = (slab > 0, slab < SLABS - 1, band > 0, band < BANDS - 1)
 
     towards = (device(dz=1), device(dz=-1))
@@ -361,16 +375,36 @@
 
     writes = []
     started = []
-    for ap in range(2):
+    def start(copy):
+        copy.start()
+        started.append(copy)
+
+    def forward(distance, half):
+        for way in range(2):
+            if distance == 1:
+                for part in range(PARTS):
+                    ring(way, 1, half * PARTS + part).wait_recv()
+            else:
+                ring(way, distance, half).wait_recv()
+            if distance < 3 or half == way:
+                start(ring(way, distance + 1, half))
+
+    def receive(ap):
         for copy in halos[ap]:
             copy.wait_recv()
         interleave(clean, xf, xi, ap, has)
-        for part in range(PARTS):
-            convolve(xi, tab, so.at[ap], waves, held, pair_sum, ap, part)
-            for way in range(2):
-                copy = ring(way, 1, ap * PARTS + part)
-                copy.start()
-                started.append(copy)
+
+    def advance(ap, part):
+        convolve(xi, tab, so.at[ap], waves, held, pair_sum, ap, part)
+        for way in range(2):
+            start(ring(way, 1, ap * PARTS + part))
+
+    receive(0)
+    advance(0, 0)
+    advance(0, 1)
+    receive(1)
+    advance(1, 0)
+    advance(1, 1)
 
     def write_signal(ap):
         sig_v[ap] = jnp.concatenate([so[ap, t] for t in range(TICKS // LANES)], axis=1).astype(BF)
@@ -397,29 +431,17 @@
             copy.wait_recv()
         place(bslot, picks, inbox, blob_ref, slot, source, core, band)
 
-    def forward(distance, half):
-        for way in range(2):
-            if distance == 1:
-                for part in range(PARTS):
-                    ring(way, 1, half * PARTS + part).wait_recv()
-            else:
-                ring(way, distance, half).wait_recv()
-            if distance < 3 or half == way:
-                copy = ring(way, distance + 1, half)
-                copy.start()
-                started.append(copy)
-
     forward(1, 0)
     for copy in asks:
         copy.wait_recv()
     serve(0, 0)
-    write_signal(0)
     forward(1, 1)
     serve(1, -1)
     serve(4, 1)
+    write_signal(0)
+    forward(2, 0)
     write_signal(1)
     blob_ref[...] = jnp.zeros_like(blob_ref)
-    forward(2, 0)
     collect(0, 0)
     forward(2, 1)
     serve(2, -2)
@@ -431,10 +453,10 @@
     serve(3, -3)
     serve(6, 3)
     collect(2, -2)
-    collect(5, 2)
     ring(0, 4, 0).wait_recv()
     ring(1, 4, 1).wait_recv()
     serve(7, 4)
+    collect(5, 2)
     collect(3, -3)
     collect(6, 3)
     collect(7, 4)
@@ -472,9 +494,12 @@
             jax.ShapeDtypeStruct((2, WIRES, TICKS), BF),
             jax.ShapeDtypeStruct((BLOBS, SLICES), F32),
         ),
-        in_specs=[pl.BlockSpec(memory_space=pl.ANY)] + [vmem] * 3,
+        in_specs=[pl.BlockSpec(memory_space=pl.ANY)] * 4,
         out_specs=(pl.BlockSpec(memory_space=pl.ANY), vmem),
         scratch_shapes=[
+            pltpu.VMEM((2, WIRES), jnp.int32),
+            pltpu.VMEM((TAPS, TICKS + 1), BF),
+            pltpu.VMEM((PLACES, BLOBS), jnp.int32),
             pltpu.VMEM((2, TALL, LONG), BF),
             pltpu.VMEM((LONG // LANES, TALL, LANES), F32),
             pltpu.VMEM((2, COLS // 2 + WR, 2, 2, 16, REACH), BF),
@@ -486,6 +511,7 @@
             pltpu.VMEM((TICKS, SLICES), BF),
             pltpu.VMEM((2, WIRES, TICKS), BF),
             pltpu.VMEM((PLANES, 2 * WIRES, SLICES), BF),
+            pltpu.VMEM((32, BLOBS), F32),
             pltpu.VMEM((PLACES * GROUPS, BLOBS), BF),
             pltpu.VMEM((PLACES * GROUPS, BLOBS), F32),
             pltpu.VMEM((BLOBS, BLOBS // 3), BF),
@@ -502,7 +528,7 @@
             dma((2, 9)),
             dma((PLANES, PEERS)),
             dma((PLANES, PEERS)),
-            dma((3,)),
+            dma((7,)),
         ],
         compiler_params=pltpu.CompilerParams(
             collective_id=0, has_side_effects=True, vmem_limit_bytes=56 << 20

time: 65.1 us -> 62.9 us (0.966)
  Pallas kernels: 64.3 us -> 62.1 us
    pallas_call x1, Pallas kernels: 62.2 us -> 60 us  [shards(): pl.pallas_call(whole, out_shape=(jax.ShapeDtypeStruct((2, WIRES, TICKS),...]
where the time goes in v5:
time: 62.9 us; the launch traced here: 62.7 us
  Pallas kernels  62.1 us (99%)
  between operations  0.64 us (1%)
    pallas_call x1, Pallas kernels, shards(): pl.pallas_call(whole, out_shape=(jax.ShapeDtypeStruct((2, WIRES, TICKS),...  60 us
    pallas_call x1, Pallas kernels, hand_over(): pl.pallas_call(body, grid=(steps,), out_shape=tuple((jax.ShapeDtypeStruct...  2.06 us

profile of v5, /device:TPU:1, one launch (start us, length us, event | category | flops | bytes accessed | tf_op | source)
XLA Modules:
  0.0 62.7 jit_solution(16017448087876776613)
XLA Ops:
  0.6 60.0 %shard_map.59 = (bf16[2,640,256]{2,1,0:T(8,128)(2,1)}, f32[768,128]{1,0:T(8,128)}) custom-call(bf16[2,640,256]{2,1,0:T(8,128)(2,1)} %raw_ref.1, s32[2,640]{1,0:T(2,128)} %mask_ref.1, bf16[21,257]{1,0:T(8,128)(2,1)} %k_ref.1, s32[12,768]{1,0:T(8,128)} %bitcast.1), custom_call_target="tpu_custom_call" | custom-call | tf_op jit(solution)/shard_map/pallas_call | solution.py:491
  60.7 2.1 %shard_map.60 = (bf16[2,640,256]{2,1,0:T(8,128)(2,1)}, f32[768,128]{1,0:T(8,128)}) custom-call(bf16[2,640,256]{2,1,0:T(8,128)(2,1)} %get-tuple-element.4.signal_in, f32[768,128]{1,0:T(8,128)} %get-tuple-element.5.charge_in), custom_call_target="tpu_custom_call" | custom-call | tf_op jit(solution)/shard_map/pallas_call | solution.py:479

commit v6 on v5

--- a/solution.py
+++ b/solution.py
@@ -178,11 +178,11 @@
 
 def make_requests(fields, request, bslot, hots, counts):
     blob = iota((1, BLOBS), 1)
-    blob_high = tall(((blob >> 7) + 1).astype(F32), GROUPS)
+    blob_high = ((blob >> 7) + 1).astype(F32)
     blob_low = tall((blob & 127).astype(F32), GROUPS)
     slot = iota((SLOTS, BLOBS), 0).astype(F32).astype(BF)
     before = jnp.zeros((GROUPS, 1), F32)
-    table = jnp.zeros((4 * GROUPS, SLOTS), F32)
+    table = jnp.zeros((3 * GROUPS, SLOTS), F32)
     for k in range(PLACES):
         here = slice(k * GROUPS, (k + 1) * GROUPS)
         hot = hots[here, :]
@@ -193,9 +193,8 @@
         slot_hot = one_if(slot == tall(rank, SLOTS))
         values = jnp.concatenate(
             [
-                hot * tall(fields[k : k + 1, :], GROUPS),
+                hot * tall(fields[k : k + 1, :] * 8.0 + blob_high, GROUPS),
                 hot * tall(fields[16 + k : 17 + k, :], GROUPS),
-                hot * blob_high,
                 hot * blob_low,
             ],
             axis=0,
@@ -203,8 +202,13 @@
         table = table + lax.dot_general(
             values, slot_hot, (((1,), (1,)), ((), ())), preferred_element_type=F32
         )
-    request[...] = jnp.transpose(table[0 : 2 * GROUPS]).astype(BF)
-    bslot[...] = table[2 * GROUPS :]
+    both = table[0:GROUPS].astype(jnp.int32)
+    row_high = (both >> 3).astype(F32)
+    request[...] = jnp.transpose(
+        jnp.concatenate([row_high, table[GROUPS : 2 * GROUPS]], axis=0)
+    ).astype(BF)
+    bslot[0:GROUPS, :] = (both & 7).astype(F32)
+    bslot[GROUPS:, :] = table[2 * GROUPS :]
 
 
 def pick(reqbox, held, picks, slot, plane, core, band):
@@ -418,7 +422,7 @@
         source = lax.rem(plane + shift + PLANES, PLANES)
         pick(reqbox, held, picks, slot, source, core, band)
         boxes[slot] = []
-        for r in range(1, PEERS):
+        for r in (2, 6, 1, 3, 5, 7, 4):
             copy = remote(
                 picks.at[slot, r], inbox.at[slot, r], box_send.at[slot, r], box_recv.at[slot, r], peers[r]
             )

time: 62.9 us -> 62.3 us (level)
  no operation moved by 1% of the time
where the time goes in v6:
time: 62.3 us; the launch traced here: 62.2 us
  Pallas kernels  61.5 us (99%)
  between operations  0.64 us (1%)
    pallas_call x1, Pallas kernels, shards(): pl.pallas_call(whole, out_shape=(jax.ShapeDtypeStruct((2, WIRES, TICKS),...  59.5 us
    pallas_call x1, Pallas kernels, hand_over(): pl.pallas_call(body, grid=(steps,), out_shape=tuple((jax.ShapeDtypeStruct...  2.06 us

profile of v6, /device:TPU:1, one launch (start us, length us, event | category | flops | bytes accessed | tf_op | source)
XLA Modules:
  0.0 62.2 jit_solution(7927796648224261485)
XLA Ops:
  0.6 59.5 %shard_map.59 = (bf16[2,640,256]{2,1,0:T(8,128)(2,1)}, f32[768,128]{1,0:T(8,128)}) custom-call(bf16[2,640,256]{2,1,0:T(8,128)(2,1)} %raw_ref.1, s32[2,640]{1,0:T(2,128)} %mask_ref.1, bf16[21,257]{1,0:T(8,128)(2,1)} %k_ref.1, s32[12,768]{1,0:T(8,128)} %bitcast.1), custom_call_target="tpu_custom_call" | custom-call | tf_op jit(solution)/shard_map/pallas_call | solution.py:495
  60.1 2.1 %shard_map.60 = (bf16[2,640,256]{2,1,0:T(8,128)(2,1)}, f32[768,128]{1,0:T(8,128)}) custom-call(bf16[2,640,256]{2,1,0:T(8,128)(2,1)} %get-tuple-element.4.signal_in, f32[768,128]{1,0:T(8,128)} %get-tuple-element.5.charge_in), custom_call_target="tpu_custom_call" | custom-call | tf_op jit(solution)/shard_map/pallas_call | solution.py:483

commit v7 on v6

--- a/solution.py
+++ b/solution.py
@@ -182,7 +182,8 @@
     blob_low = tall((blob & 127).astype(F32), GROUPS)
     slot = iota((SLOTS, BLOBS), 0).astype(F32).astype(BF)
     before = jnp.zeros((GROUPS, 1), F32)
-    table = jnp.zeros((3 * GROUPS, SLOTS), F32)
+    all_values = []
+    slot_hots = []
     for k in range(PLACES):
         here = slice(k * GROUPS, (k + 1) * GROUPS)
         hot = hots[here, :]
@@ -190,7 +191,7 @@
         count = counts[here, :]
         rank = jnp.sum(hot32 * (count + before), axis=0, keepdims=True)
         before = before + (count + hot32)[:, BLOBS - 1 : BLOBS]
-        slot_hot = one_if(slot == tall(rank, SLOTS))
+        slot_hots.append(one_if(slot == tall(rank, SLOTS)))
         values = jnp.concatenate(
             [
                 hot * tall(fields[k : k + 1, :] * 8.0 + blob_high, GROUPS),
@@ -199,9 +200,13 @@
             ],
             axis=0,
         )
-        table = table + lax.dot_general(
-            values, slot_hot, (((1,), (1,)), ((), ())), preferred_element_type=F32
-        )
+        all_values.append(values)
+    table = lax.dot_general(
+        jnp.concatenate(all_values, axis=1),
+        jnp.concatenate(slot_hots, axis=1),
+        (((1,), (1,)), ((), ())),
+        preferred_element_type=F32,
+    )
     both = table[0:GROUPS].astype(jnp.int32)
     row_high = (both >> 3).astype(F32)
     request[...] = jnp.transpose(

time: 62.3 us -> 62.3 us (level)
  no operation moved by 1% of the time
where the time goes in v7:
time: 62.3 us; the launch traced here: 62.2 us
  Pallas kernels  61.5 us (99%)
  between operations  0.64 us (1%)
    pallas_call x1, Pallas kernels, shards(): pl.pallas_call(whole, out_shape=(jax.ShapeDtypeStruct((2, WIRES, TICKS),...  59.5 us
    pallas_call x1, Pallas kernels, hand_over(): pl.pallas_call(body, grid=(steps,), out_shape=tuple((jax.ShapeDtypeStruct...  2.06 us

profile of v7, /device:TPU:1, one launch (start us, length us, event | category | flops | bytes accessed | tf_op | source)
XLA Modules:
  0.0 62.2 jit_solution(3978850118890544248)
XLA Ops:
  0.6 59.5 %shard_map.59 = (bf16[2,640,256]{2,1,0:T(8,128)(2,1)}, f32[768,128]{1,0:T(8,128)}) custom-call(bf16[2,640,256]{2,1,0:T(8,128)(2,1)} %raw_ref.1, s32[2,640]{1,0:T(2,128)} %mask_ref.1, bf16[21,257]{1,0:T(8,128)(2,1)} %k_ref.1, s32[12,768]{1,0:T(8,128)} %bitcast.1), custom_call_target="tpu_custom_call" | custom-call | tf_op jit(solution)/shard_map/pallas_call | solution.py:500
  60.1 2.1 %shard_map.60 = (bf16[2,640,256]{2,1,0:T(8,128)(2,1)}, f32[768,128]{1,0:T(8,128)}) custom-call(bf16[2,640,256]{2,1,0:T(8,128)(2,1)} %get-tuple-element.4.signal_in, f32[768,128]{1,0:T(8,128)} %get-tuple-element.5.charge_in), custom_call_target="tpu_custom_call" | custom-call | tf_op jit(solution)/shard_map/pallas_call | solution.py:488
